TPU v7x, 32 devices: a whole 2x2x4 slice. The times are simulated.
32 devices in a mesh: row: 2 (over x), col: 8 (over z, y), depth: 2 (over core).
Axes of the slice: x: 2, y: 2, z: 4, core: 2. Of those that a mesh axis runs over, the one named last changes fastest.
Arguments:
- activations: bfloat16 [2, 512, 8192], P('depth', 'col', 'row'), may hold values from -6 to 6
- weight_tiles: bfloat16 [2, 8, 448, 128, 128], P('row', 'col'), may hold values from -0.09375 to 0.09375
- tile_rows: int32 [2, 8, 448], P('row', 'col'), may hold values from 0 to 31, as said below
- tile_cols: int32 [2, 8, 448], P('row', 'col'), may hold values from 0 to 27, as said below
- grad_out: bfloat16 [2, 512, 28672], P('depth', 'row', 'col'), may hold values from -6 to 6
Outputs:
- output: bfloat16 [2, 512, 28672], P('depth', 'row', 'col')
- grad_input: bfloat16 [2, 512, 8192], P('depth', 'col', 'row')
- grad_tiles: float32 [2, 8, 448, 128, 128], P('row', 'col')
Inputs may be any that keep to these rules, and one draw needn't show every extreme that they name: For each block (i, j), the pairs (tile_rows[i, j, k], tile_cols[i, j, k]) over k are 448 distinct tiles of the block's 32 x 28 grid, in increasing order of tile_rows * 28 + tile_cols. `tile_cols`: drawn together with tile_rows, as stated there.
All inputs are finite; a program needn't handle non-finite values.
Results may differ from a plain program's by a relative error of at most 0.001.
Values may be sent and summed in bfloat16 or wider, within the bound.
No kernel may reach another device: no remote copies, remote signals or barrier semaphores. Data moves between devices by JAX's collectives and lax.ppermute only.
A program may use at most 256 MiB of HBM per device.

v0:
```python
import math

import jax
import jax.numpy as jnp
from jax import lax
from jax.sharding import PartitionSpec as P

TILE_SIZE = 128


def kept_products(left, right, rows_here, cols_here, count_rows, count_cols):
    total_rows = left.shape[0]

    def one_block(left_part, right_part):
        part_rows = left_part.shape[0]
        left_kept = jnp.take(left_part.reshape(part_rows, count_rows, TILE_SIZE), rows_here, axis=1)
        right_kept = jnp.take(
            right_part.reshape(part_rows, count_cols, TILE_SIZE), cols_here, axis=1
        )
        return jnp.einsum("tkb,tkj->kbj", left_kept, right_kept, preferred_element_type=jnp.float32)

    block_size = 512
    if total_rows > block_size and total_rows % block_size == 0:
        steps_count = total_rows // block_size
        left_blocks = left.reshape(steps_count, block_size, left.shape[1])
        right_blocks = right.reshape(steps_count, block_size, right.shape[1])

        def add_block(carry, pair):
            return (carry + one_block(pair[0], pair[1]), None)

        start_value = jnp.zeros((rows_here.shape[0], TILE_SIZE, TILE_SIZE), jnp.float32)
        summed, unused = lax.scan(add_block, start_value, (left_blocks, right_blocks))
        return summed
    return one_block(left, right)


def shards(activations, weight_tiles, tile_rows, tile_cols, grad_out):
    kept_weights = weight_tiles[0, 0]
    rows_here = tile_rows[0, 0]
    cols_here = tile_cols[0, 0]
    width_rows = activations.shape[2]
    width_cols = grad_out.shape[2]
    count_rows = width_rows // TILE_SIZE
    count_cols = width_cols // TILE_SIZE
    tile_grid = jnp.zeros((count_rows, count_cols, TILE_SIZE, TILE_SIZE), jnp.bfloat16)
    tile_grid = tile_grid.at[rows_here, cols_here].set(kept_weights)
    dense_block = tile_grid.transpose(0, 2, 1, 3).reshape(width_rows, width_cols)
    gathered = lax.all_gather(activations[0], "col", axis=0, tiled=True)
    group_tokens = gathered.shape[0]
    segment = gathered
    out_rows = lax.psum_scatter(
        jnp.dot(segment, dense_block, preferred_element_type=jnp.float32),
        "row",
        scatter_dimension=0,
        tiled=True,
    )
    output = out_rows.astype(jnp.bfloat16)[None]
    grad_tokens = lax.all_gather(grad_out[0], "row", axis=0, tiled=True)
    segment = grad_tokens
    input_rows = lax.psum_scatter(
        lax.dot_general(
            segment, dense_block, (((1,), (1,)), ((), ())), preferred_element_type=jnp.float32
        ),
        "col",
        scatter_dimension=0,
        tiled=True,
    )
    grad_input = input_rows.astype(jnp.bfloat16)[None]
    grad_scale = math.sqrt(group_tokens * lax.axis_size("depth"))
    local_grad = kept_products(gathered, grad_tokens, rows_here, cols_here, count_rows, count_cols)
    summed_grad = lax.psum(local_grad, "depth")
    grad_tiles = (summed_grad / grad_scale)[None, None]
    return (output, grad_input, grad_tiles)


def solution(mesh):
    placed = (
        P("depth", "col", "row"),
        P("row", "col", None, None, None),
        P("row", "col", None),
        P("row", "col", None),
        P("depth", "row", "col"),
    )
    return jax.shard_map(
        shards,
        mesh=mesh,
        in_specs=placed,
        out_specs=(
            P("depth", "row", "col"),
            P("depth", "col", "row"),
            P("row", "col", None, None, None),
        ),
        check_vma=False,
    )
```

profile of v0, /device:TPU:0, one launch (start us, length us, event | category | flops | bytes accessed | tf_op | source)
XLA Modules:
  0.0 533.2 jit_solution(7229536686447907813)
XLA Ops:
  7.2 3.8 copy.25
  11.1 0.7 all-gather.5.cloned.1.call-update
  11.8 0.7 compare_select_fusion.1
  12.6 10.8 %broadcast_in_dim.32 = bf16[32,28,128,128]{3,2,1,0:T(8,128)(2,1)} broadcast(bf16[]{:T(256)} %constant.19.clone.1), dimensions={} | broadcast | bytes 29360130 | tf_op jit(solution)/shard_map/broadcast_in_dim | solution.py:45
  23.3 71.3 %scatter_fusion = bf16[32,28,128,128]{3,2,1,0:T(8,128)(2,1)} fusion(bf16[32,28,128,128]{3,2,1,0:T(8,128)(2,1)} %broadcast_in_dim.32, s32[448]{0:T(512)S(1)} %bitcast.64, bf16[448,128,128]{2,1,0:T(8,128)(2,1)} %bitcast.66), kind=kCustom, calls=%fused_computation.2 | custom fusion | bytes 44043776 | tf_op jit(solution)/shard_map/scatter | solution.py:46
  94.6 38.8 %copy.24 = bf16[32,128,28,128]{1,0,3,2:T(8,128)(2,1)} copy(bf16[32,128,28,128]{3,1,2,0:T(8,128)(2,1)} %bitcast.61) | data formatting | bytes 58720256 | tf_op jit(solution)/shard_map/transpose | solution.py:47
  133.4 25.7 %fusion.17 = f32[512,4096]{0,1:T(8,128)} fusion(bf16[448,8,32,128]{3,2,1,0:T(8,128)(2,1)} %bitcast.62, bf16[1,512,3584]{1,2,0:T(8,128)(2,1)} %all-gather.7.cloned.1.call-done), kind=kOutput, calls=%fused_computation.19 | convolution fusion | flops 15032385536 | bytes 41418752 | tf_op jit(solution)/shard_map/dot_general | solution.py:61
  159.2 9.0 %copy.33 = f32[512,4096]{1,0:T(8,128)} copy(f32[512,4096]{0,1:T(8,128)} %fusion.17) | data formatting | bytes 16777216
  168.4 24.1 %fusion.14 = f32[512,3584]{0,1:T(8,128)} fusion(bf16[448,8,32,128]{3,2,1,0:T(8,128)(2,1)} %bitcast.63, bf16[1,512,4096]{2,1,0:T(8,128)(2,1)} %all-gather.5.cloned.1.call-done), kind=kOutput, calls=%fused_computation.18 | convolution fusion | flops 15032385536 | bytes 40894464 | tf_op jit(solution)/shard_map/dot_general | solution.py:52
  192.6 0.3 all-reduce.2.cloned.1.call-start
  192.9 6.0 %copy.28 = bf16[512,28,128]{2,0,1:T(8,128)(2,1)} copy(bf16[512,28,128]{0,2,1:T(8,128)(2,1)} %bitcast.68) | data formatting | bytes 7340032 | tf_op jit(solution)/shard_map/reshape | solution.py:18
  198.9 24.4 %gather_fusion.1 = bf16[448,512,128]{2,1,0:T(8,128)(2,1)} fusion(bf16[512,28,128]{2,0,1:T(8,128)(2,1)} %copy.28, s32[1024]{0:T(1024)S(1)} %pad_clamp_fusion), kind=kCustom, calls=%fused_computation.1 | custom fusion | bytes 117442304 | tf_op jit(solution)/shard_map/jit(_take)/gather | solution.py:17
  223.3 6.4 %copy.26 = bf16[1,512,4096]{1,2,0:T(8,128)(2,1)} copy(bf16[1,512,4096]{2,1,0:T(8,128)(2,1)} %all-gather.5.cloned.1.call-done) | data formatting | bytes 8388608 | tf_op jit(solution)/shard_map/all_gather | solution.py:48
  229.7 6.5 %copy.27 = bf16[512,32,128]{2,0,1:T(8,128)(2,1)} copy(bf16[512,32,128]{0,2,1:T(8,128)(2,1)} %bitcast.65) | data formatting | bytes 8388608 | tf_op jit(solution)/shard_map/reshape | solution.py:16
  236.2 24.6 %gather_fusion = bf16[448,512,128]{2,1,0:T(8,128)(2,1)} fusion(bf16[512,32,128]{2,0,1:T(8,128)(2,1)} %copy.27, s32[1024]{0:T(1024)S(1)} %pad_clamp_fusion.1), kind=kCustom, calls=%fused_computation | custom fusion | bytes 117442304 | tf_op jit(solution)/shard_map/jit(_take)/gather | solution.py:16
  260.9 48.5 %fusion = f32[448,128,128]{2,1,0:T(8,128)} fusion(bf16[448,512,128]{2,1,0:T(8,128)(2,1)} %gather_fusion.1, bf16[448,512,128]{2,1,0:T(8,128)(2,1)} %gather_fusion, pred[448]{0:T(512)(128)(4,1)S(1)} %get-tuple-element.18, pred[448]{0:T(512)(128)(4,1)S(1)} %get-tuple-element.19), kind=kOutput, calls=%fused_computation.3 | convolution fusion | flops 7574913024 | bytes 146801536 | tf_op jit(solution)/shard_map/tkb,tkj->kbj/dot_general | solution.py:20
  309.4 9.1 %reduce-scatter.7.cloned.1.call-done = f32[64,4096]{1,0:T(8,128)} async-done(((f32[512,4096]{1,0:T(8,128)}), f32[64,4096]{1,0:T(8,128)}) %reduce-scatter.7.cloned.1.call-update) | async-done | bytes 1048592
  318.5 1.7 copy.34
  320.2 1.1 copy.31
  321.3 87.0 %reduce-scatter.5.cloned.1.call-done = f32[256,3584]{0,1:T(8,128)} async-done(((f32[512,3584]{0,1:T(8,128)}), f32[256,3584]{0,1:T(8,128)}) %reduce-scatter.5.cloned.1.call-update) | async-done | bytes 3670032 | tf_op jit(solution)/shard_map/reduce_scatter | solution.py:51
  408.3 2.2 convert_bitcast_fusion
  410.5 2.6 copy.30
  413.1 91.5 %all-reduce.2.cloned.1.call-done = f32[448,128,128]{2,1,0:T(8,128)} async-done(((f32[448,128,128]{2,1,0:T(8,128)}), f32[448,128,128]{2,1,0:T(8,128)}) %all-reduce.2.cloned.1.call-update) | async-done | bytes 29360144 | tf_op jit(solution)/shard_map/psum | solution.py:71
  504.6 22.1 %multiply_bitcast_fusion = f32[1,1,448,128,128]{4,3,2,1,0:T(8,128)} fusion(f32[448,128,128]{2,1,0:T(8,128)} %all-reduce.2.cloned.1.call-done), kind=kLoop, calls=%fused_computation.15 | loop fusion | flops 7340032 | bytes 58720256 | tf_op jit(solution)/shard_map/broadcast_in_dim | solution.py:72
  (17 shorter events, 0.5 us)
Async XLA Ops:
  7.2 126.3 %all-gather.7.cloned.1.call-start = ((), (), s32[]{:S(2)}) async-start(), calls=%async_computation.5 | async-start | bytes 5505024 | tf_op jit(solution)/shard_map/all_gather | solution.py:58
  11.0 157.4 %all-gather.5.cloned.1.call-start = ((), (), s32[]{:S(2)}) async-start(), calls=%async_computation.4 | async-start | bytes 4718592 | tf_op jit(solution)/shard_map/all_gather | solution.py:48
  11.8 306.7 %reduce-scatter.7.cloned.1.call-start = ((), (), s32[]{:S(2)}) async-start(), calls=%async_computation.6 | async-start | bytes 9437184
  168.2 24.7 %copy-start = (s32[1,1,448]{2,1,0:T(1,128)S(1)}, s32[1,1,448]{2,1,0:T(1,128)}, u32[]{:S(2)}) copy-start(s32[1,1,448]{2,1,0:T(1,128)} %param.7) | copy-start | bytes 5380
  168.2 24.7 %copy-start.1 = (s32[1,1,448]{2,1,0:T(1,128)S(1)}, s32[1,1,448]{2,1,0:T(1,128)}, u32[]{:S(2)}) copy-start(s32[1,1,448]{2,1,0:T(1,128)} %param.8) | copy-start | bytes 5380
  168.2 240.1 %reduce-scatter.5.cloned.1.call-start = ((), (), s32[]{:S(2)}) async-start(), calls=%async_computation.2 | async-start | bytes 11010048 | tf_op jit(solution)/shard_map/reduce_scatter | solution.py:51
  192.6 312.0 %all-reduce.2.cloned.1.call-start = ((), (), s32[]{:S(2)}) async-start(), calls=%async_computation.3 | async-start | bytes 58720256 | tf_op jit(solution)/shard_map/psum | solution.py:71
Sparse Core Ops, SparseCore 0:
  11.2 53.4 all-gather.6
  66.8 72.8 all-gather.4
  168.3 150.1 reduce-scatter.6
  320.7 87.6 reduce-scatter.4
  411.2 93.3 all-reduce.1
where the time goes:
time: 536 us; the launch traced here: 533 us
  local copies, waits for them, and re-layouts  207 us (39%)
  waiting for transfers between devices  188 us (35%)
  matrix products  98.3 us (18%)
  other arithmetic  25 us (5%)
  between operations  13.9 us (3%)
    psum x1, waiting for transfers between devices, shards(): summed_grad = lax.psum(local_grad, 'depth')  91.5 us
    reduce_scatter x1, waiting for transfers between devices, shards(): lax.psum_scatter(jnp.dot(segment, dense_block, preferred_element_type=jnp...  87 us
    scatter x1, local copies, waits for them, and re-layouts, shards(): tile_grid = tile_grid.at[rows_here, cols_here].set(kept_weights)  71.3 us
    dot_general x1, matrix products, one_block(): jnp.einsum('tkb,tkj->kbj', left_kept, right_kept, preferred_element_type=...  48.5 us
    transpose x1, local copies, waits for them, and re-layouts, shards(): tile_grid.transpose(0, 2, 1, 3).reshape(width_rows, width_cols)  38.8 us
    dot_general x1, matrix products, shards(): lax.dot_general(segment, dense_block, (((1,), (1,)), ((), ())), preferred...  25.7 us
    gather x1, local copies, waits for them, and re-layouts, one_block(): jnp.take(left_part.reshape(part_rows, count_rows, TILE_SIZE), rows_here,...  24.6 us
    gather x1, local copies, waits for them, and re-layouts, one_block(): jnp.take(right_part.reshape(part_rows, count_cols, TILE_SIZE), cols_here,...  24.4 us
  transfers between devices with their start and end apart: 5, of which 3 were waited for; matrix products, arithmetic and copies ran while one was open for 57% of the time, Pallas kernels for 0%

commit v1 on v0

v1 whole, which is shorter than its diff:
```python
import math

import jax
import jax.numpy as jnp
from jax import lax
from jax.experimental import pallas as pl
from jax.experimental.pallas import tpu as pltpu
from jax.sharding import PartitionSpec as P


TILE = 128
GROUP = 2 * TILE
LANES = 128
CHUNK = 32
OUT_CHUNK = 16
LEVELS = 32600.0
SMALL = 1e-30
VMEM_LIMIT = 56 * 1024 * 1024


def params(limit=VMEM_LIMIT):
    return pltpu.CompilerParams(vmem_limit_bytes=limit)


def encode(values):
    top = jnp.maximum(jnp.max(jnp.abs(values), axis=1, keepdims=True), SMALL)
    eighths = jnp.ceil(8.0 * jnp.log2(top * (1.0 / LEVELS)))
    codes = jnp.round(values * jnp.exp2(eighths * -0.125)).astype(jnp.int32).astype(jnp.int16)
    return codes, eighths


def decode(codes, eighths):
    return codes.astype(jnp.int32).astype(jnp.float32) * jnp.exp2(eighths * 0.125)


def lane_of(shape):
    return lax.broadcasted_iota(jnp.int32, shape, len(shape) - 1)


def pick_lane(values, lane):
    values = values.astype(jnp.int32).astype(jnp.float32)
    return jnp.sum(jnp.where(lane_of(values.shape) == lane, values, 0.0), axis=1, keepdims=True)


def put_lane(values, column, lane):
    return jnp.where(lane_of(values.shape) == lane, column, values)


def pack(values):
    return values.astype(jnp.int32).astype(jnp.int16)


def strip_matmul(blocks, order, weight, count_rows, count_cols, along_rows, coded, kept, gathered, instead=None):
    builds = isinstance(weight, tuple)
    outer_tiles = count_rows if along_rows else count_cols
    width = GROUP * 2 if outer_tiles % 4 == 0 else GROUP
    per = width // TILE
    steps = outer_tiles // per
    inner = (count_cols if along_rows else count_rows) * TILE
    outer = outer_tiles * TILE
    tokens = sum(rows for _, rows, _ in blocks)
    first_kept = tokens - kept
    strip_shape = (width, inner) if along_rows else (inner, width)
    spots = 0
    meta = order
    if builds:
        tiles, places, ends = weight
        kept_tiles = tiles.shape[0]
        chunk = CHUNK if kept_tiles % CHUNK == 0 else kept_tiles
        chunks = kept_tiles // chunk
        ends = (ends[per - 1 :: per] + (chunk - 1)) // chunk
        meta = jnp.concatenate([places.reshape(-1), jnp.zeros((1,), jnp.int32), ends, order])
        spots = count_rows * count_cols + 1 + steps

    def kernel(meta, *refs):
        ins, refs = refs[: len(blocks)], refs[len(blocks) :]
        weight_ref, refs = refs[0], refs[1:]
        if instead:
            instead_ref, refs = refs[0], refs[1:]
        if coded:
            codes_ref, refs = refs[0], refs[1:]
        if kept:
            kept_ref, refs = refs[0], refs[1:]
        if gathered:
            gathered_ref, refs = refs[0], refs[1:]
        if builds:
            built_ref, refs = refs[0], refs[1:]
        held, refs = refs[0], refs[1:]
        step = pl.program_id(0)

        @pl.when(step == 0)
        def _():
            held[...] = jnp.zeros_like(held)

        def mixed(here, there):
            rows = coded // len(instead[2])
            out = []
            for (a, n), (b, m) in instead[2]:
                one, two = (v[i * rows : (i + 1) * rows] for v, i in (((here, there)[a], n), ((here, there)[b], m)))
                out.append(jnp.where(meta[spots + instead[1]] == 1, one, two))
            return jnp.concatenate(out, axis=0)

        if builds:
            local, sems = refs

            def chunk_copy(n):
                here = pl.ds(n * chunk, chunk)
                return pltpu.make_async_copy(weight_ref.at[here], local.at[here], sems.at[n])

            @pl.when(step == 0)
            def _():
                for n in range(chunks):
                    chunk_copy(n).start()
                local[kept_tiles] = jnp.zeros((TILE, TILE), jnp.bfloat16)

            base = count_rows * count_cols
            lax.fori_loop(meta[base + step], meta[base + step + 1], lambda n, c: (chunk_copy(n).wait(), c)[1], 0)

            @pl.when(step == steps - 1)
            def _():
                lax.fori_loop(meta[base + step + 1], chunks, lambda n, c: (chunk_copy(n).wait(), c)[1], 0)

            for a in range(per):
                for c in range(count_cols):
                    tile = meta[(step * per + a) * count_cols + c]
                    built_ref[a * TILE : (a + 1) * TILE, c * TILE : (c + 1) * TILE] = local[tile]
            strip = built_ref[...]
        else:
            strip = weight_ref[...]
        x = jnp.concatenate([r[...] for r in ins], axis=0) if len(ins) > 1 else ins[0][...]
        if along_rows:
            y = lax.dot_general(x, strip, (((1,), (1,)), ((), ())), preferred_element_type=jnp.float32)
        else:
            y = jnp.dot(x, strip, preferred_element_type=jnp.float32)
        if coded:
            for g in range(width // GROUP):
                codes, eighths = encode(y[:coded, g * GROUP : (g + 1) * GROUP])
                here = pl.ds(pl.multiple_of(step * width + g * GROUP, GROUP), GROUP)
                if instead:
                    codes = mixed(codes, instead_ref[:, here])
                codes_ref[:, here] = codes
                held[...] = put_lane(held[...], eighths, step * (width // GROUP) + g)

            @pl.when(step == steps - 1)
            def _():
                last = pack(held[...])
                if instead:
                    last = mixed(last, instead_ref[:, outer:])
                codes_ref[:, outer:] = last

        if kept:
            kept_ref[...] = y[first_kept:]
        if gathered:

            @pl.when(step == 0)
            def _():
                gathered_ref[...] = x

    def in_spec(rows, entry):
        def place(step, meta):
            return (0 if entry is None else meta[spots + entry], 0)

        return pl.BlockSpec((rows, inner), place, pipeline_mode=pl.Buffered(1))

    outs, out_specs = [], []
    if coded:
        outs.append(jax.ShapeDtypeStruct((coded, outer + LANES), jnp.int16))
        out_specs.append(pl.BlockSpec((coded, outer + LANES), lambda s, m: (0, 0)))
    if kept:
        outs.append(jax.ShapeDtypeStruct((kept, outer), jnp.float32))
        out_specs.append(pl.BlockSpec((kept, width), lambda s, m: (0, s)))
    if gathered:
        outs.append(jax.ShapeDtypeStruct((tokens, inner), jnp.bfloat16))
        out_specs.append(pl.BlockSpec((tokens, inner), lambda s, m: (0, 0)))
    scratch = [pltpu.VMEM((max(coded, 8), LANES), jnp.float32)]
    strip_spec = pl.BlockSpec(strip_shape, (lambda s, m: (s, 0)) if along_rows else (lambda s, m: (0, s)))
    if builds:
        outs.append(jax.ShapeDtypeStruct((count_rows * TILE, count_cols * TILE), jnp.bfloat16))
        out_specs.append(strip_spec)
        strip_spec = pl.BlockSpec(memory_space=pl.ANY)
        scratch += [pltpu.VMEM((kept_tiles + 1, TILE, TILE), jnp.bfloat16), pltpu.SemaphoreType.DMA((chunks,))]
    return pl.pallas_call(
        kernel,
        out_shape=outs,
        grid_spec=pltpu.PrefetchScalarGridSpec(
            num_scalar_prefetch=1,
            grid=(steps,),
            in_specs=[in_spec(rows, entry) for _, rows, entry in blocks]
            + [strip_spec]
            + ([pl.BlockSpec((coded, outer + LANES), lambda s, m: (0, 0), pipeline_mode=pl.Buffered(1))] * bool(instead)),
            out_specs=out_specs,
            scratch_shapes=scratch,
        ),
        compiler_params=params(),
        cost_estimate=pl.CostEstimate(
            flops=2 * tokens * inner * outer,
            bytes_accessed=inner * outer * 2 + tokens * (inner * 2 + outer * 4),
            transcendentals=0,
        ),
        name="dgrad" if along_rows else "forward",
    )(meta, *[a for a, _, _ in blocks], tiles if builds else weight, *([instead[0]] if instead else []))


def tile_products(lefts, rights, order, places, ends, kept_tiles, count_rows, count_cols, factor, part, before):
    tokens = sum(rows * len(entries) for _, rows, entries in lefts)
    first, count = part
    wide_rows, wide_cols = count * TILE, count_cols * TILE
    per = 4 if count % 4 == 0 else 2
    cols_per = 4 if count_cols % 4 == 0 else 2
    row_steps, col_steps = count // per, count_cols // cols_per
    spots = count_rows * count_cols
    meta = jnp.concatenate([places.reshape(-1), jnp.zeros((1,), jnp.int32), ends, order])
    copies = sum(len(e) for _, _, e in lefts) + sum(len(e) for _, _, e in rights)

    def kernel(meta, *refs):
        left_refs, refs = refs[: len(lefts)], refs[len(lefts) :]
        right_refs, refs = refs[: len(rights)], refs[len(rights) :]
        if before is not None:
            refs = refs[1:]
        out_ref, left_all, right_all, turned, found, in_sems, out_sems = refs
        i, j = pl.program_id(0), pl.program_id(1)

        def input_copies():
            n = 0
            for group, group_refs, whole, cols in (
                (lefts, left_refs, left_all, pl.ds(first * TILE, wide_rows)),
                (rights, right_refs, right_all, pl.ds(0, wide_cols)),
            ):
                for (_, rows, entries), ref in zip(group, group_refs):
                    for b, entry in enumerate(entries):
                        to = pl.multiple_of(meta[spots + 1 + count_rows + entry] * rows, rows)
                        yield pltpu.make_async_copy(
                            ref.at[pl.ds(b * rows, rows), cols], whole.at[pl.ds(to, rows), :], in_sems.at[n]
                        )
                        n += 1

        @pl.when((i == 0) & (j == 0))
        def _():
            for c in input_copies():
                c.start()
            for c in input_copies():
                c.wait()
            turned[0] = left_all[:, : per * TILE].T

        now = lax.rem(i, 2)
        cols = pl.ds(pl.multiple_of(j * cols_per * TILE, cols_per * TILE), cols_per * TILE)
        sums = jnp.dot(turned[now], right_all[:, cols], preferred_element_type=jnp.float32) * factor
        for a in range(per):
            for b in range(cols_per):
                tile = meta[(first + i * per + a) * count_cols + j * cols_per + b]
                found[tile] = sums[a * TILE : (a + 1) * TILE, b * TILE : (b + 1) * TILE]
        piece = lax.rem(j, per)
        ahead = jnp.minimum(i + 1, row_steps - 1) * per + piece
        turned[1 - now, pl.ds(pl.multiple_of(piece * TILE, TILE), TILE), :] = left_all[
            :, pl.ds(pl.multiple_of(ahead * TILE, TILE), TILE)
        ].T

        def out_copies(low, high, begin):
            many = (high - low) // OUT_CHUNK

            def copy(at, size, sem):
                c = pltpu.make_async_copy(found.at[pl.ds(at, size)], out_ref.at[pl.ds(at, size)], sem)
                c.start() if begin else c.wait()

            def chunk(n, c):
                copy(low + n * OUT_CHUNK, OUT_CHUNK, out_sems.at[0])
                return c

            def single(n, c):
                copy(n, 1, out_sems.at[1])
                return c

            lax.fori_loop(0, many, chunk, 0)
            lax.fori_loop(low + many * OUT_CHUNK, high, single, 0)

        def bounds(n):
            row = spots + first + n * per
            return meta[row], meta[row + per]

        @pl.when(j == col_steps - 1)
        def _():
            out_copies(*bounds(i), True)

        @pl.when((i == row_steps - 1) & (j == col_steps - 1))
        def _():
            for n in range(row_steps):
                out_copies(*bounds(n), False)

    operands = [a for a, _, _ in lefts] + [a for a, _, _ in rights]
    aliases = {}
    if before is not None:
        aliases = {1 + len(operands): 0}
        operands.append(before)
    return pl.pallas_call(
        kernel,
        out_shape=jax.ShapeDtypeStruct((kept_tiles, TILE, TILE), jnp.float32),
        grid_spec=pltpu.PrefetchScalarGridSpec(
            num_scalar_prefetch=1,
            grid=(row_steps, col_steps),
            in_specs=[pl.BlockSpec(memory_space=pl.ANY)] * len(operands),
            out_specs=pl.BlockSpec(memory_space=pl.ANY),
            scratch_shapes=[
                pltpu.VMEM((tokens, wide_rows), jnp.bfloat16),
                pltpu.VMEM((tokens, wide_cols), jnp.bfloat16),
                pltpu.VMEM((2, per * TILE, tokens), jnp.bfloat16),
                pltpu.VMEM((kept_tiles + 1, TILE, TILE), jnp.float32),
                pltpu.SemaphoreType.DMA((copies,)),
                pltpu.SemaphoreType.DMA((2,)),
            ],
        ),
        input_output_aliases=aliases,
        compiler_params=params(),
        cost_estimate=pl.CostEstimate(
            flops=2 * tokens * wide_rows * wide_cols,
            bytes_accessed=tokens * (wide_rows + wide_cols) * 2
            + kept_tiles * TILE * TILE * 4 * count // count_rows,
            transcendentals=0,
        ),
        name="wgrad",
    )(meta, *operands)


def add_received(terms, order, rows, wide, sends, keeps, keep_type):
    span = 1024 if wide % 1024 == 0 else wide
    steps, groups = wide // span, span // GROUP

    def kernel(meta, *refs):
        ins, refs = refs[: 3 * len(terms)], refs[3 * len(terms) :]
        if sends:
            codes_ref, refs = refs[0], refs[1:]
        keep_ref, held = refs
        step = pl.program_id(0)

        @pl.when(step == 0)
        def _():
            held[...] = jnp.zeros_like(held)

        for g in range(groups):
            here = slice(g * GROUP, (g + 1) * GROUP)
            there = pl.ds(pl.multiple_of(step * span + g * GROUP, GROUP), GROUP)
            sums = []
            for p in range(len(terms)):
                local, codes, last = ins[3 * p : 3 * p + 3]
                eighths = pick_lane(last[...], step * groups + g)
                sums.append(local[:, here] + decode(codes[:, here], eighths))
            for n, keep in enumerate(keeps):
                keep_ref[n * rows : (n + 1) * rows, here] = keep(sums, meta).astype(keep_type)
            for n, send in enumerate(sends):
                codes, eighths = encode(send(sums, meta))
                codes_ref[n * rows : (n + 1) * rows, there] = codes
                held[n] = put_lane(held[n], eighths, step * groups + g)

        @pl.when(step == steps - 1)
        def _():
            for n in range(len(sends)):
                codes_ref[n * rows : (n + 1) * rows, wide:] = pack(held[n])

    in_specs, operands = [], []
    for local, local_entry, codes, entry in terms:
        in_specs += [
            pl.BlockSpec((rows, span), lambda s, m, e=local_entry: (m[e], s)),
            pl.BlockSpec((rows, span), lambda s, m, e=entry: (m[e], s)),
            pl.BlockSpec((rows, LANES), lambda s, m, e=entry: (m[e], wide // LANES)),
        ]
        operands += [local, codes, codes]
    outs, out_specs = [], []
    if sends:
        outs.append(jax.ShapeDtypeStruct((len(sends) * rows, wide + LANES), jnp.int16))
        out_specs.append(pl.BlockSpec((len(sends) * rows, wide + LANES), lambda s, m: (0, 0)))
    outs.append(jax.ShapeDtypeStruct((len(keeps) * rows, wide), keep_type))
    out_specs.append(pl.BlockSpec((len(keeps) * rows, span), lambda s, m: (0, s)))
    return pl.pallas_call(
        kernel,
        out_shape=outs,
        grid_spec=pltpu.PrefetchScalarGridSpec(
            num_scalar_prefetch=1,
            grid=(steps,),
            in_specs=in_specs,
            out_specs=out_specs,
            scratch_shapes=[pltpu.VMEM((max(len(sends), 1), rows, LANES), jnp.float32)],
        ),
        compiler_params=params(),
        cost_estimate=pl.CostEstimate(
            flops=8 * rows * wide, bytes_accessed=len(terms) * rows * wide * 10, transcendentals=0
        ),
        name="add_received",
    )(order, *operands)


def tile_places(tile_rows, tile_cols, count_rows, count_cols):
    kept = tile_rows.shape[0]
    position = tile_rows * count_cols + tile_cols
    short = jnp.arange(kept, dtype=jnp.int32) - kept
    spot = jnp.arange(count_rows * count_cols, dtype=jnp.int32)
    places = jnp.sum(jnp.where(position[None, :] == spot[:, None], short[None, :], 0), axis=1) + kept
    rows = jnp.arange(count_rows, dtype=jnp.int32)
    ends = jnp.sum((tile_rows[None, :] <= rows[:, None]).astype(jnp.int32), axis=1)
    return places, ends


def shards_general(activations, weight_tiles, tile_rows, tile_cols, grad_out):
    tiles = weight_tiles[0, 0]
    count_rows = activations.shape[2] // TILE
    count_cols = grad_out.shape[2] // TILE
    places, ends = tile_places(tile_rows[0, 0], tile_cols[0, 0], count_rows, count_cols)
    none = jnp.arange(2, dtype=jnp.int32)
    act = lax.all_gather(activations[0], "col", axis=0, tiled=True)
    grad = lax.all_gather(grad_out[0], "row", axis=0, tiled=True)
    tokens = act.shape[0]
    build = (tiles, places, ends)
    back, weight = strip_matmul([(grad, tokens, None)], none, build, count_rows, count_cols, True, 0, tokens, False)
    (partial,) = strip_matmul([(act, tokens, None)], none, weight, count_rows, count_cols, False, 0, tokens, False)
    output = lax.psum_scatter(partial, "row", scatter_dimension=0, tiled=True).astype(jnp.bfloat16)[None]
    grad_input = lax.psum_scatter(back, "col", scatter_dimension=0, tiled=True).astype(jnp.bfloat16)[None]
    groups = lax.axis_size("depth")
    all_act = lax.all_gather(act, "depth", axis=0, tiled=True)
    all_grad = lax.all_gather(grad, "depth", axis=0, tiled=True)
    grad_tiles = tile_products(
        [(all_act, tokens * groups, [0])],
        [(all_grad, tokens * groups, [0])],
        none,
        places,
        ends,
        tiles.shape[0],
        count_rows,
        count_cols,
        1.0 / math.sqrt(tokens * groups),
        (0, count_rows),
        None,
    )
    return output, grad_input, grad_tiles[None, None]


def swap(value, axis, bit, size):
    return lax.ppermute(value, axis, [(i, i ^ bit) for i in range(size)])


def shards_paired(activations, weight_tiles, tile_rows, tile_cols, grad_out):
    tiles = weight_tiles[0, 0]
    count_rows = activations.shape[2] // TILE
    count_cols = grad_out.shape[2] // TILE
    wide_rows = activations.shape[2]
    size = lax.axis_size("col")
    row, col = lax.axis_index("row"), lax.axis_index("col")
    y, z0, z1 = col % 2, col // 2 % 2, col // 4
    block = activations.shape[1]
    half = grad_out.shape[1]
    places, ends = tile_places(tile_rows[0, 0], tile_cols[0, 0], count_rows, count_cols)

    def swap_col(value, bit):
        return swap(value, "col", bit, size)

    def swap_depth(value):
        return swap(value, "depth", 1, 2)

    def swap_row(value):
        return swap(value, "row", 1, 2)

    grad_mine = grad_out[0]
    own = activations[0]
    grad_other = swap_row(grad_mine)
    b2 = swap_col(own, 2)
    b6 = swap_col(own, 6)
    b1 = swap_col(own, 1)
    b3 = swap_col(b2, 1)
    b4 = swap_col(b6, 2)
    b7 = swap_col(b6, 1)
    b5 = swap_col(b4, 1)
    send_near = (z1 != row).astype(jnp.int32)

    def dgrad(grad, weight):
        blocks = [(grad, block, e) for e in range(4)]
        order = jnp.stack([1 - y, 3 - y, y, 2 + y]).astype(jnp.int32)
        return strip_matmul(blocks, order, weight, count_rows, count_cols, True, 2 * block, 2 * block, False)

    def forward(blocks, weight, instead):
        blocks = [(b, block, None) for b in blocks]
        order = send_near[None]
        return strip_matmul(blocks, order, weight, count_rows, count_cols, False, half, half, True, instead)

    first_set, second_set = (0, 1, 2, 6), (3, 4, 5, 7)
    codes_mine, kept_mine, weight = dgrad(grad_mine, (tiles, places, ends))
    codes_mine = swap_col(codes_mine, 1)
    first_codes, first_kept, first_act = forward([own, b1, b2, b6], weight, None)
    codes_other, kept_other = dgrad(grad_other, weight)
    codes_other = swap_col(codes_other, 1)
    pairs = []
    for n in range(4):
        pairs.append(
            tuple((1, first_set.index(k)) if k in first_set else (0, second_set.index(k)) for k in (n, n + 4))
        )
    out_codes, second_kept, second_act = forward([b3, b4, b5, b7], weight, (first_codes, 0, pairs))
    out_codes = swap_row(out_codes)

    order = jnp.stack([z0, 1 - z0, (z1 == row).astype(jnp.int32), 0 * z0, 0 * z0 + 1]).astype(jnp.int32)
    terms = [
        (kept, e, codes, e) for kept, codes in ((kept_mine, codes_mine), (kept_other, codes_other)) for e in (0, 1)
    ]
    codes, kept = add_received(
        terms,
        order,
        block,
        wide_rows,
        [lambda s, m: s[1], lambda s, m: s[3]],
        [lambda s, m: s[0], lambda s, m: s[2]],
        jnp.float32,
    )
    codes = swap_col(codes, 2)

    groups = lax.axis_size("depth")
    partner = [swap_depth(v) for v in (first_act, second_act, grad_mine, grad_other)]
    places_order = [g * size + (col ^ k) for g in range(groups) for k in first_set + second_set]
    places_order += [2 * g + (row if k == 0 else 1 - row) for g in range(groups) for k in range(2)]
    places_order = jnp.stack(places_order).astype(jnp.int32)
    lefts = [(v, block, [4 * n + k for k in range(4)]) for n, v in enumerate((first_act, second_act, *partner[:2]))]
    rights = [(v, half, [groups * size + n]) for n, v in enumerate((grad_mine, grad_other, *partner[2:]))]

    def wgrad(part, before):
        return tile_products(
            lefts,
            rights,
            places_order,
            places,
            ends,
            tiles.shape[0],
            count_rows,
            count_cols,
            1.0 / math.sqrt(size * block * groups),
            part,
            before,
        )

    middle = count_rows // 2
    grad_tiles = wgrad((0, middle), None)
    terms = [(kept, 3, codes, 3), (kept, 4, codes, 4)]
    codes, kept = add_received(
        terms,
        order,
        block,
        wide_rows,
        [lambda s, m: jnp.where(m[2] == 1, s[1], s[0])],
        [lambda s, m: jnp.where(m[2] == 1, s[0], s[1])],
        jnp.float32,
    )
    codes = swap_col(codes, 4)
    grad_tiles = wgrad((middle, count_rows - middle), grad_tiles)
    (grad_input,) = add_received([(kept, 3, codes, 3)], order, block, wide_rows, [], [lambda s, m: s[0]], jnp.bfloat16)
    output = join_output(first_kept, second_kept, pairs, out_codes, send_near, col, block)
    return output[None], grad_input[None], grad_tiles[None, None]


def join_output(first, second, pairs, codes, send_near, col, rows):
    wide = first.shape[1]
    blocks = first.shape[0] // rows
    order = jnp.arange(blocks, dtype=jnp.int32) ^ (col % blocks)
    table = jnp.array([[[1 - p[w][0] for p in pairs], [p[w][1] for p in pairs]] for w in (0, 1)], jnp.int32)
    table = jnp.where(send_near == 1, table[1], table[0])
    chosen, index = (jnp.sum(jnp.where(order[:, None] == jnp.arange(blocks), t[None], 0), axis=1) for t in table)
    meta = jnp.concatenate([order, chosen, jnp.where(chosen == 1, 0, index), jnp.where(chosen == 1, index, 0)])
    meta = meta.astype(jnp.int32)

    def kernel(meta, first_ref, second_ref, codes_ref, out_ref):
        use_second = meta[blocks + pl.program_id(0)] == 1
        for g in range(wide // GROUP):
            here = slice(g * GROUP, (g + 1) * GROUP)
            local = jnp.where(use_second, second_ref[:, here], first_ref[:, here])
            eighths = pick_lane(codes_ref[:, wide:], g)
            out_ref[:, here] = (local + decode(codes_ref[:, here], eighths)).astype(jnp.bfloat16)

    return pl.pallas_call(
        kernel,
        out_shape=jax.ShapeDtypeStruct((blocks * rows, wide), jnp.bfloat16),
        grid_spec=pltpu.PrefetchScalarGridSpec(
            num_scalar_prefetch=1,
            grid=(blocks,),
            in_specs=[
                pl.BlockSpec((rows, wide), lambda n, m: (m[2 * blocks + n], 0)),
                pl.BlockSpec((rows, wide), lambda n, m: (m[3 * blocks + n], 0)),
                pl.BlockSpec((rows, wide + LANES), lambda n, m: (m[n], 0)),
            ],
            out_specs=pl.BlockSpec((rows, wide), lambda n, m: (n, 0)),
        ),
        compiler_params=params(),
        cost_estimate=pl.CostEstimate(flops=8 * first.size, bytes_accessed=first.size * 8, transcendentals=0),
        name="join_output",
    )(meta, first, second, codes)


def solution(mesh):
    specs = (
        P("depth", "col", "row"),
        P("row", "col", None, None, None),
        P("row", "col", None),
        P("row", "col", None),
        P("depth", "row", "col"),
    )
    paired = mesh.shape["row"] == 2 and mesh.shape["col"] == 8 and mesh.shape["depth"] == 2

    def body(*args):
        return (shards_paired if paired else shards_general)(*args)

    return jax.shard_map(
        body,
        mesh=mesh,
        in_specs=specs,
        out_specs=(specs[4], specs[0], specs[1]),
        check_vma=False,
    )
```

time: 536 us -> 253 us (0.47)
  local copies, waits for them, and re-layouts: 207 us -> 5.38 us
  Pallas kernels: 0 us -> 153 us
  waiting for transfers between devices: 188 us -> 62.7 us
  matrix products: 98.3 us -> 0 us
  starting transfers between devices: 0.6 us -> 27.1 us
  other arithmetic: 25 us -> 3.14 us
  between operations: 13.9 us -> 0.8 us
    pallas_call x0 -> x10, Pallas kernels: none -> 153 us  [the longest x4 73.7 us: strip_matmul(): pl.pallas_call(kernel, out_shape=outs, grid_spec=pltpu.PrefetchScalarGrid...]
    dot_general x3 -> x0, matrix products: 98.3 us -> none  [the longest x1 48.5 us: one_block(): jnp.einsum('tkb,tkj->kbj', left_kept, right_kept, preferred_element_type=...]
    psum x1 -> x0, waiting for transfers between devices: 91.5 us -> none  [shards(): summed_grad = lax.psum(local_grad, 'depth')]
    reduce_scatter x1 -> x0, waiting for transfers between devices: 87 us -> none  [shards(): lax.psum_scatter(jnp.dot(segment, dense_block, preferred_element_type=jnp...]
    scatter x1 -> x0, local copies, waits for them, and re-layouts: 71.3 us -> none  [shards(): tile_grid = tile_grid.at[rows_here, cols_here].set(kept_weights)]
    ppermute x0 -> x17, waiting for transfers between devices: none -> 62.7 us  [swap(): return lax.ppermute(value, axis, [(i, i ^ bit) for i in range(size)])]
    gather x2 -> x0, local copies, waits for them, and re-layouts: 49.1 us -> none  [the longest x1 24.6 us: one_block(): jnp.take(left_part.reshape(part_rows, count_rows, TILE_SIZE), rows_here,...]
    transpose x1 -> x0, local copies, waits for them, and re-layouts: 38.8 us -> none  [shards(): tile_grid.transpose(0, 2, 1, 3).reshape(width_rows, width_cols)]
  transfers between devices with their start and end apart: 5 -> 17, of which waited for: 3 -> 5; matrix products, arithmetic and copies ran while one was open for 57% -> 2% of each run, Pallas kernels for 0% -> 57%
where the time goes in v1:
time: 253 us; the launch traced here: 252 us
  Pallas kernels  153 us (60%)
  waiting for transfers between devices  62.7 us (25%)
  starting transfers between devices  27.1 us (11%)
  local copies, waits for them, and re-layouts  5.38 us (2%)
  other arithmetic  3.14 us (1%)
    pallas_call x4, Pallas kernels, strip_matmul(): pl.pallas_call(kernel, out_shape=outs, grid_spec=pltpu.PrefetchScalarGrid...  73.7 us
    ppermute x17, waiting for transfers between devices, swap(): return lax.ppermute(value, axis, [(i, i ^ bit) for i in range(size)])  62.7 us
    pallas_call x2, Pallas kernels, tile_products(): pl.pallas_call(kernel, out_shape=jax.ShapeDtypeStruct((kept_tiles, TILE,...  57.2 us
    ppermute x17, starting transfers between devices, swap(): return lax.ppermute(value, axis, [(i, i ^ bit) for i in range(size)])  27.1 us
    pallas_call x3, Pallas kernels, add_received(): pl.pallas_call(kernel, out_shape=outs, grid_spec=pltpu.PrefetchScalarGrid...  15.9 us
    pallas_call x1, Pallas kernels, join_output(): pl.pallas_call(kernel, out_shape=jax.ShapeDtypeStruct((blocks * rows, wid...  5.78 us
  transfers between devices with their start and end apart: 17, of which 5 were waited for; matrix products, arithmetic and copies ran while one was open for 2% of the time, Pallas kernels for 57%

profile of v1, /device:TPU:0, one launch (start us, length us, event | category | flops | bytes accessed | tf_op | source)
XLA Modules:
  0.0 251.7 jit_solution(17109157063203510942)
XLA Ops:
  0.6 3.0 %collective-permute-start.9 = (bf16[256,3584]{1,0:T(8,128)(2,1)}, bf16[256,3584]{1,0:T(8,128)(2,1)S(1)}, u32[]{:S(2)}, u32[]{:S(2)}) collective-permute-start(bf16[256,3584]{1,0:T(8,128)(2,1)} %bitcast.10.refs_0_.refs_1_.refs_2_.refs_3_.refs_4_), channel_id=1, source_target_pairs={{0,16},{16,0},{1,17},{17,1},{2,18},{18,2},{3,19},{19,3},{4,20},{20... | collective-permute-start | bytes 5505032 | tf_op jit(solution)/shard_map/ppermute | solution.py:435
  3.7 3.6 %collective-permute-start.2 = (bf16[64,4096]{1,0:T(8,128)(2,1)}, bf16[64,4096]{1,0:T(8,128)(2,1)}, u32[]{:S(2)}, u32[]{:S(2)}) collective-permute-start(bf16[64,4096]{1,0:T(8,128)(2,1)} %bitcast.42), channel_id=1, source_target_pairs={{0,12},{2,14},{4,8},{6,10},{8,4},{10,6},{12,0},{14,2},{1,13},{3,15... | collective-permute-start | bytes 1572872 | tf_op jit(solution)/shard_map/ppermute | solution.py:435
  7.3 1.5 collective-permute-start
  11.3 9.3 %collective-permute-done.2.refs_3_ = bf16[64,4096]{1,0:T(8,128)(2,1)} collective-permute-done((bf16[64,4096]{1,0:T(8,128)(2,1)}, bf16[64,4096]{1,0:T(8,128)(2,1)}, u32[]{:S(2)}, u32[]{:S(2)}) %collective-permute-start.2) | collective-permute-done | bytes 524320 | tf_op jit(solution)/shard_map/ppermute | solution.py:435
  20.6 9.6 %collective-permute-start.4 = (bf16[64,4096]{1,0:T(8,128)(2,1)}, bf16[64,4096]{1,0:T(8,128)(2,1)}, u32[]{:S(2)}, u32[]{:S(2)}) collective-permute-start(bf16[64,4096]{1,0:T(8,128)(2,1)} %collective-permute-done.2.refs_3_), channel_id=1, source_target_pairs={{0,4},{2,6},{4,0},{6,2},{8,12},{10,14},{12,8},{14,10},{1,5},{3,7},... | collective-permute-start | bytes 1572872 | tf_op jit(solution)/shard_map/ppermute | solution.py:435
  30.2 19.0 %dgrad.2 = (s16[128,4224]{1,0:T(8,128)(2,1)}, f32[128,4096]{1,0:T(8,128)}, bf16[4096,3584]{1,0:T(8,128)(2,1)}) custom-call(s32[909]{0:T(1024)} %concatenate.13.meta, bf16[256,3584]{1,0:T(8,128)(2,1)} %bitcast.10.refs_0_.refs_1_.refs_2_.refs_3_.refs_4_, bf16[256,3584]{1,0:T(8,128)(2,1)} %bitcast.10.refs_0_.refs_1_.refs_2_.refs_3_.refs_4_, ...), custom_call_target="tpu_custom_call" | custom-call | flops 7516192768 | bytes 35389440 | tf_op jit(solution)/shard_map/dgrad/pallas_call | solution.py:182
  49.2 1.6 collective-permute-start.8
  51.9 1.5 collective-permute-start.3
  54.6 17.6 %dgrad.3 = (s16[128,4224]{1,0:T(8,128)(2,1)}, f32[128,4096]{1,0:T(8,128)}) custom-call(s32[4]{0:T(128)} %pad_add_fusion.1.meta, bf16[256,3584]{1,0:T(8,128)(2,1)} %copy-done, bf16[256,3584]{1,0:T(8,128)(2,1)} %copy-done, bf16[256,3584]{1,0:T(8,128)(2,1)} %copy-done, bf16[256,3584]{1,0:T(8,128)(2,1)} %copy-done, bf16[4096,3584]{1,0:T(8,128)(2,1)} %get-tuple-element.18.refs_4_), custom_call_target="tpu_custom_call" | custom-call | flops 7516192768 | bytes 35389440 | tf_op jit(solution)/shard_map/dgrad/pallas_call | solution.py:182
  72.3 0.9 collective-permute-start.10
  73.1 18.1 %forward.2 = (s16[256,3712]{1,0:T(8,128)(2,1)}, f32[256,3584]{1,0:T(8,128)}, bf16[256,4096]{1,0:T(8,128)(2,1)}) custom-call(s32[1]{0:T(128)} %bitcast.2.meta, bf16[64,4096]{1,0:T(8,128)(2,1)} %bitcast.45, bf16[64,4096]{1,0:T(8,128)(2,1)} %collective-permute-done.refs_1_, bf16[64,4096]{1,0:T(8,128)(2,1)} %copy-done.5, ...), custom_call_target="tpu_custom_call" | custom-call | flops 7516192768 | bytes 35127296 | tf_op jit(solution)/shard_map/forward/pallas_call | solution.py:182
  91.3 7.3 %collective-permute-done.3.refs_0_ = bf16[64,4096]{1,0:T(8,128)(2,1)S(1)} collective-permute-done((bf16[64,4096]{1,0:T(8,128)(2,1)S(1)}, bf16[64,4096]{1,0:T(8,128)(2,1)S(1)}, u32[]{:S(2)}, u32[]{:S(2)}) %collective-permute-start.3) | collective-permute-done | bytes 524320 | tf_op jit(solution)/shard_map/ppermute | solution.py:435
  98.7 11.2 %collective-permute-done.5.refs_2_ = bf16[64,4096]{1,0:T(8,128)(2,1)S(1)} collective-permute-done((bf16[64,4096]{1,0:T(8,128)(2,1)}, bf16[64,4096]{1,0:T(8,128)(2,1)S(1)}, u32[]{:S(2)}, u32[]{:S(2)}) %collective-permute-start.5) | collective-permute-done | bytes 524320 | tf_op jit(solution)/shard_map/ppermute | solution.py:435
  110.7 18.9 %forward.3 = (s16[256,3712]{1,0:T(8,128)(2,1)}, f32[256,3584]{1,0:T(8,128)}, bf16[256,4096]{1,0:T(8,128)(2,1)}) custom-call(s32[1]{0:T(128)} %bitcast.2.meta, bf16[64,4096]{1,0:T(8,128)(2,1)} %copy-done.7, bf16[64,4096]{1,0:T(8,128)(2,1)} %collective-permute-done.4.refs_1_, bf16[64,4096]{1,0:T(8,128)(2,1)} %copy-done.8, bf16[64,4096]{1,0:T(8,128)(2,1)} %copy-done.6, ...), custom_call_target="tpu_custom_call" | custom-call | flops 7516192768 | bytes 35127296 | tf_op jit(solution)/shard_map/forward/pallas_call | solution.py:182
  133.2 6.5 %add_received.3 = (s16[128,4224]{1,0:T(8,128)(2,1)}, f32[128,4096]{1,0:T(8,128)}) custom-call(s32[5]{0:T(128)} %stack.103.meta, f32[128,4096]{1,0:T(8,128)} %get-tuple-element.23.refs_0_.refs_3_, s16[128,4224]{1,0:T(8,128)(2,1)} %copy-done.2, s16[128,4224]{1,0:T(8,128)(2,1)} %copy-done.2, f32[128,4096]{1,0:T(8,128)} %get-tuple-element.23.refs_0_.refs_3_, ...), custom_call_target="tpu_custom_call" | custom-call | flops 2097152 | bytes 10485760 | tf_op jit(solution)/shard_map/add_received/pallas_call | solution.py:372
  139.6 34.1 %collective-permute-done.7.codes_ref = s16[256,3712]{1,0:T(8,128)(2,1)} collective-permute-done((s16[256,3712]{1,0:T(8,128)(2,1)}, s16[256,3712]{1,0:T(8,128)(2,1)}, u32[]{:S(2)}, u32[]{:S(2)}) %collective-permute-start.7) | collective-permute-done | bytes 1900576 | tf_op jit(solution)/shard_map/ppermute | solution.py:435
  173.8 5.8 %join_output.1 = bf16[256,3584]{1,0:T(8,128)(2,1)} custom-call(s32[16]{0:T(128)} %pad_add_fusion.meta, f32[256,3584]{1,0:T(8,128)} %get-tuple-element.19.first_ref, f32[256,3584]{1,0:T(8,128)} %get-tuple-element.21.second_ref, s16[256,3712]{1,0:T(8,128)(2,1)} %collective-permute-done.7.codes_ref), custom_call_target="tpu_custom_call" | custom-call | flops 7340032 | bytes 7340032 | tf_op jit(solution)/shard_map/join_output/pallas_call | solution.py:570
  179.6 28.6 %wgrad.2.refs_8_ = f32[448,128,128]{2,1,0:T(8,128)} custom-call(s32[949]{0:T(1024)} %concatenate.14.meta, bf16[256,4096]{1,0:T(8,128)(2,1)} %get-tuple-element.31.refs_0_, bf16[256,4096]{1,0:T(8,128)(2,1)} %get-tuple-element.32.refs_1_, bf16[256,4096]{1,0:T(8,128)(2,1)} %collective-permute-done.13.refs_2_, ...), custom_call_target="tpu_custom_call" | custom-call | flops 15032385536 | bytes 26214400 | tf_op jit(solution)/shard_map/wgrad/pallas_call | solution.py:294
  208.3 1.0 copy-done.3
  209.3 5.2 %add_received.4 = (s16[64,4224]{1,0:T(8,128)(2,1)}, f32[64,4096]{1,0:T(8,128)}) custom-call(s32[5]{0:T(128)} %stack.103.meta, f32[128,4096]{1,0:T(8,128)} %get-tuple-element.27.refs_0_.refs_3_, s16[128,4224]{1,0:T(8,128)(2,1)} %copy-done.3, s16[128,4224]{1,0:T(8,128)(2,1)} %copy-done.3, f32[128,4096]{1,0:T(8,128)} %get-tuple-element.27.refs_0_.refs_3_, ...), custom_call_target="tpu_custom_call" | custom-call | flops 2097152 | bytes 5242880 | tf_op jit(solution)/shard_map/add_received/pallas_call | solution.py:372
  214.4 3.6 %collective-permute-start.12 = (s16[64,4224]{1,0:T(8,128)(2,1)}, s16[64,4224]{1,0:T(8,128)(2,1)S(1)}, u32[]{:S(2)}, u32[]{:S(2)}) collective-permute-start(s16[64,4224]{1,0:T(8,128)(2,1)} %get-tuple-element.30), channel_id=1, source_target_pairs={{0,8},{2,10},{4,12},{6,14},{8,0},{10,2},{12,4},{14,6},{1,9},{3,11}... | collective-permute-start | bytes 1622024 | tf_op jit(solution)/shard_map/ppermute | solution.py:435
  218.0 28.6 %wgrad.3 = f32[448,128,128]{2,1,0:T(8,128)} custom-call(s32[949]{0:T(1024)} %concatenate.14.meta, bf16[256,4096]{1,0:T(8,128)(2,1)} %get-tuple-element.31.refs_0_, bf16[256,4096]{1,0:T(8,128)(2,1)} %get-tuple-element.32.refs_1_, bf16[256,4096]{1,0:T(8,128)(2,1)} %collective-permute-done.13.refs_2_, ...), custom_call_target="tpu_custom_call", output_to_operand_aliasing={{}: (9, {})} | custom-call | flops 15032385536 | bytes 26214400 | tf_op jit(solution)/shard_map/wgrad/pallas_call | solution.py:294
  246.7 0.8 copy-done.4
  247.5 4.2 %add_received.5 = bf16[64,4096]{1,0:T(8,128)(2,1)} custom-call(s32[5]{0:T(128)} %stack.103.meta, f32[64,4096]{1,0:T(8,128)} %get-tuple-element.29.refs_0_, s16[64,4224]{1,0:T(8,128)(2,1)} %copy-done.4, s16[64,4224]{1,0:T(8,128)(2,1)} %copy-done.4), custom_call_target="tpu_custom_call" | custom-call | flops 2097152 | bytes 2621440 | tf_op jit(solution)/shard_map/add_received/pallas_call | solution.py:372
  (58 shorter events, 9.3 us)
Async XLA Ops:
  0.6 52.8 %collective-permute-start.9 = (bf16[256,3584]{1,0:T(8,128)(2,1)}, bf16[256,3584]{1,0:T(8,128)(2,1)S(1)}, u32[]{:S(2)}, u32[]{:S(2)}) collective-permute-start(bf16[256,3584]{1,0:T(8,128)(2,1)} %bitcast.10.refs_0_.refs_1_.refs_2_.refs_3_.refs_4_), channel_id=1, source_target_pairs={{0,16},{16,0},{1,17},{17,1},{2,18},{18,2},{3,19},{19,3},{4,20},{20... | collective-permute-start | bytes 5505032 | tf_op jit(solution)/shard_map/ppermute | solution.py:435
  3.7 17.0 %collective-permute-start.2 = (bf16[64,4096]{1,0:T(8,128)(2,1)}, bf16[64,4096]{1,0:T(8,128)(2,1)}, u32[]{:S(2)}, u32[]{:S(2)}) collective-permute-start(bf16[64,4096]{1,0:T(8,128)(2,1)} %bitcast.42), channel_id=1, source_target_pairs={{0,12},{2,14},{4,8},{6,10},{8,4},{10,6},{12,0},{14,2},{1,13},{3,15... | collective-permute-start | bytes 1572872 | tf_op jit(solution)/shard_map/ppermute | solution.py:435
  7.3 44.1 %collective-permute-start.1 = (bf16[64,4096]{1,0:T(8,128)(2,1)}, bf16[64,4096]{1,0:T(8,128)(2,1)S(1)}, u32[]{:S(2)}, u32[]{:S(2)}) collective-permute-start(bf16[64,4096]{1,0:T(8,128)(2,1)} %bitcast.43), channel_id=1, source_target_pairs={{0,4},{2,6},{4,0},{6,2},{8,12},{10,14},{12,8},{14,10},{1,5},{3,7},... | collective-permute-start | bytes 1572872 | tf_op jit(solution)/shard_map/ppermute | solution.py:435
  7.3 65.0 %collective-permute-start = (bf16[64,4096]{1,0:T(8,128)(2,1)}, bf16[64,4096]{1,0:T(8,128)(2,1)}, u32[]{:S(2)}, u32[]{:S(2)}) collective-permute-start(bf16[64,4096]{1,0:T(8,128)(2,1)} %bitcast.44), channel_id=1, source_target_pairs={{0,2},{2,0},{4,6},{6,4},{8,10},{10,8},{12,14},{14,12},{1,3},{3,1},... | collective-permute-start | bytes 1572872 | tf_op jit(solution)/shard_map/ppermute | solution.py:435
  20.6 31.3 %collective-permute-start.4 = (bf16[64,4096]{1,0:T(8,128)(2,1)}, bf16[64,4096]{1,0:T(8,128)(2,1)}, u32[]{:S(2)}, u32[]{:S(2)}) collective-permute-start(bf16[64,4096]{1,0:T(8,128)(2,1)} %collective-permute-done.2.refs_3_), channel_id=1, source_target_pairs={{0,4},{2,6},{4,0},{6,2},{8,12},{10,14},{12,8},{14,10},{1,5},{3,7},... | collective-permute-start | bytes 1572872 | tf_op jit(solution)/shard_map/ppermute | solution.py:435
  49.2 81.1 %collective-permute-start.8 = (s16[128,4224]{1,0:T(8,128)(2,1)}, s16[128,4224]{1,0:T(8,128)(2,1)S(1)}, u32[]{:S(2)}, u32[]{:S(2)}) collective-permute-start(s16[128,4224]{1,0:T(8,128)(2,1)} %get-tuple-element.24), channel_id=1, source_target_pairs={{0,2},{2,0},{4,6},{6,4},{8,10},{10,8},{12,14},{14,12},{1,3},{3,1},... | collective-permute-start | bytes 3244040 | tf_op jit(solution)/shard_map/ppermute | solution.py:435
  51.4 20.9 %copy-start.5 = (bf16[64,4096]{1,0:T(8,128)(2,1)}, bf16[64,4096]{1,0:T(8,128)(2,1)S(1)}, u32[]{:S(2)}) copy-start(bf16[64,4096]{1,0:T(8,128)(2,1)S(1)} %collective-permute-done.1.refs_2_) | copy-start | bytes 1572868
  51.4 39.9 %collective-permute-start.6 = (bf16[64,4096]{1,0:T(8,128)(2,1)}, bf16[64,4096]{1,0:T(8,128)(2,1)S(1)}, u32[]{:S(2)}, u32[]{:S(2)}) collective-permute-start(bf16[64,4096]{1,0:T(8,128)(2,1)} %collective-permute-done.2.refs_3_), channel_id=1, source_target_pairs={{0,2},{2,0},{4,6},{6,4},{8,10},{10,8},{12,14},{14,12},{1,3},{3,1},... | collective-permute-start | bytes 1572872 | tf_op jit(solution)/shard_map/ppermute | solution.py:435
  51.9 46.8 %collective-permute-start.3 = (bf16[64,4096]{1,0:T(8,128)(2,1)S(1)}, bf16[64,4096]{1,0:T(8,128)(2,1)S(1)}, u32[]{:S(2)}, u32[]{:S(2)}) collective-permute-start(bf16[64,4096]{1,0:T(8,128)(2,1)S(1)} %collective-permute-done.1.refs_2_), channel_id=1, source_target_pairs={{0,2},{2,0},{4,6},{6,4},{8,10},{10,8},{12,14},{14,12},{1,3},{3,1},... | collective-permute-start | bytes 1572872 | tf_op jit(solution)/shard_map/ppermute | solution.py:435
  53.4 56.5 %collective-permute-start.5 = (bf16[64,4096]{1,0:T(8,128)(2,1)}, bf16[64,4096]{1,0:T(8,128)(2,1)S(1)}, u32[]{:S(2)}, u32[]{:S(2)}) collective-permute-start(bf16[64,4096]{1,0:T(8,128)(2,1)} %collective-permute-done.4.refs_1_), channel_id=1, source_target_pairs={{0,2},{2,0},{4,6},{6,4},{8,10},{10,8},{12,14},{14,12},{1,3},{3,1},... | collective-permute-start | bytes 1572872 | tf_op jit(solution)/shard_map/ppermute | solution.py:435
  72.3 58.9 %collective-permute-start.10 = (s16[128,4224]{1,0:T(8,128)(2,1)}, s16[128,4224]{1,0:T(8,128)(2,1)}, u32[]{:S(2)}, u32[]{:S(2)}) collective-permute-start(s16[128,4224]{1,0:T(8,128)(2,1)} %get-tuple-element.26), channel_id=1, source_target_pairs={{0,2},{2,0},{4,6},{6,4},{8,10},{10,8},{12,14},{14,12},{1,3},{3,1},... | collective-permute-start | bytes 3244040 | tf_op jit(solution)/shard_map/ppermute | solution.py:435
  91.3 18.7 %copy-start.6 = (bf16[64,4096]{1,0:T(8,128)(2,1)}, bf16[64,4096]{1,0:T(8,128)(2,1)S(1)}, u32[]{:S(2)}) copy-start(bf16[64,4096]{1,0:T(8,128)(2,1)S(1)} %collective-permute-done.6.refs_3_) | copy-start | bytes 1572868
  91.3 88.3 %collective-permute-start.13 = (bf16[256,4096]{1,0:T(8,128)(2,1)}, bf16[256,4096]{1,0:T(8,128)(2,1)}, u32[]{:S(2)}, u32[]{:S(2)}) collective-permute-start(bf16[256,4096]{1,0:T(8,128)(2,1)} %get-tuple-element.31.refs_0_), channel_id=1, source_target_pairs={{0,1},{1,0},{2,3},{3,2},{4,5},{5,4},{6,7},{7,6},{8,9},{9,8},{10,11... | collective-permute-start | bytes 6291464 | tf_op jit(solution)/shard_map/ppermute | solution.py:435
  98.7 11.2 %copy-start.7 = (bf16[64,4096]{1,0:T(8,128)(2,1)}, bf16[64,4096]{1,0:T(8,128)(2,1)S(1)}, u32[]{:S(2)}) copy-start(bf16[64,4096]{1,0:T(8,128)(2,1)S(1)} %collective-permute-done.3.refs_0_) | copy-start | bytes 1572868
  110.7 20.4 %copy-start.1 = (bf16[256,3584]{1,0:T(8,128)(2,1)S(1)}, bf16[256,3584]{1,0:T(8,128)(2,1)}, u32[]{:S(2)}) copy-start(bf16[256,3584]{1,0:T(8,128)(2,1)} %copy-done) | copy-start | bytes 5505028
  110.7 21.7 %copy-start.9 = (s32[1,2,4]{2,1,0:T(2,128)S(1)}, s32[1,2,4]{2,1,0:T(2,128)}, u32[]{:S(2)}) copy-start(s32[1,2,4]{2,1,0:T(2,128)} %constant.102) | copy-start | bytes 100
  110.7 21.7 %copy-start.10 = (s32[1,2,4]{2,1,0:T(2,128)S(1)}, s32[1,2,4]{2,1,0:T(2,128)}, u32[]{:S(2)}) copy-start(s32[1,2,4]{2,1,0:T(2,128)} %constant.101) | copy-start | bytes 100
  129.6 50.0 %collective-permute-start.14 = (bf16[256,4096]{1,0:T(8,128)(2,1)}, bf16[256,4096]{1,0:T(8,128)(2,1)}, u32[]{:S(2)}, u32[]{:S(2)}) collective-permute-start(bf16[256,4096]{1,0:T(8,128)(2,1)} %get-tuple-element.32.refs_1_), channel_id=1, source_target_pairs={{0,1},{1,0},{2,3},{3,2},{4,5},{5,4},{6,7},{7,6},{8,9},{9,8},{10,11... | collective-permute-start | bytes 6291464 | tf_op jit(solution)/shard_map/ppermute | solution.py:435
  129.7 44.1 %collective-permute-start.7 = (s16[256,3712]{1,0:T(8,128)(2,1)}, s16[256,3712]{1,0:T(8,128)(2,1)}, u32[]{:S(2)}, u32[]{:S(2)}) collective-permute-start(s16[256,3712]{1,0:T(8,128)(2,1)} %get-tuple-element.22), channel_id=1, source_target_pairs={{0,16},{16,0},{1,17},{17,1},{2,18},{18,2},{3,19},{19,3},{4,20},{20... | collective-permute-start | bytes 5701640 | tf_op jit(solution)/shard_map/ppermute | solution.py:435
  130.2 2.9 %copy-start.2 = (s16[128,4224]{1,0:T(8,128)(2,1)}, s16[128,4224]{1,0:T(8,128)(2,1)S(1)}, u32[]{:S(2)}) copy-start(s16[128,4224]{1,0:T(8,128)(2,1)S(1)} %collective-permute-done.8.refs_1_.refs_2_.refs_4_.refs_5_) | copy-start | bytes 3244036
  130.2 49.3 %collective-permute-start.15 = (bf16[256,3584]{1,0:T(8,128)(2,1)}, bf16[256,3584]{1,0:T(8,128)(2,1)}, u32[]{:S(2)}, u32[]{:S(2)}) collective-permute-start(bf16[256,3584]{1,0:T(8,128)(2,1)} %bitcast.10.refs_0_.refs_1_.refs_2_.refs_3_.refs_4_), channel_id=1, source_target_pairs={{0,1},{1,0},{2,3},{3,2},{4,5},{5,4},{6,7},{7,6},{8,9},{9,8},{10,11... | collective-permute-start | bytes 5505032 | tf_op jit(solution)/shard_map/ppermute | solution.py:435
  131.1 48.5 %collective-permute-start.16 = (bf16[256,3584]{1,0:T(8,128)(2,1)S(1)}, bf16[256,3584]{1,0:T(8,128)(2,1)}, u32[]{:S(2)}, u32[]{:S(2)}) collective-permute-start(bf16[256,3584]{1,0:T(8,128)(2,1)S(1)} %copy-done.1), channel_id=1, source_target_pairs={{0,1},{1,0},{2,3},{3,2},{4,5},{5,4},{6,7},{7,6},{8,9},{9,8},{10,11... | collective-permute-start | bytes 5505032 | tf_op jit(solution)/shard_map/ppermute | solution.py:435
  173.8 34.5 %collective-permute-start.11 = (s16[128,4224]{1,0:T(8,128)(2,1)}, s16[128,4224]{1,0:T(8,128)(2,1)S(1)}, u32[]{:S(2)}, u32[]{:S(2)}) collective-permute-start(s16[128,4224]{1,0:T(8,128)(2,1)} %get-tuple-element.28), channel_id=1, source_target_pairs={{0,4},{2,6},{4,0},{6,2},{8,12},{10,14},{12,8},{14,10},{1,5},{3,7},... | collective-permute-start | bytes 3244040 | tf_op jit(solution)/shard_map/ppermute | solution.py:435
  214.4 32.2 %collective-permute-start.12 = (s16[64,4224]{1,0:T(8,128)(2,1)}, s16[64,4224]{1,0:T(8,128)(2,1)S(1)}, u32[]{:S(2)}, u32[]{:S(2)}) collective-permute-start(s16[64,4224]{1,0:T(8,128)(2,1)} %get-tuple-element.30), channel_id=1, source_target_pairs={{0,8},{2,10},{4,12},{6,14},{8,0},{10,2},{12,4},{14,6},{1,9},{3,11}... | collective-permute-start | bytes 1622024 | tf_op jit(solution)/shard_map/ppermute | solution.py:435
  (4 other events, 3.8 us)

commit v2 on v1

v2 whole, which is shorter than its diff:
```python
import math

import jax
import jax.numpy as jnp
import numpy as np
from jax import lax
from jax.experimental import pallas as pl
from jax.experimental.pallas import tpu as pltpu
from jax.sharding import PartitionSpec as P


TILE = 128
GROUP = 2 * TILE
LANES = 128
WHOLE = 12582912.0
CHUNK = 32
OUT_CHUNK = 16
LEVELS = 32600.0
SMALL = 1e-30
VMEM_LIMIT = 63 * 1024 * 1024


def params(limit=VMEM_LIMIT):
    return pltpu.CompilerParams(vmem_limit_bytes=limit)


def encode(values):
    top = jnp.maximum(jnp.max(jnp.abs(values), axis=1, keepdims=True), SMALL)
    eighths = jnp.ceil(8.0 * jnp.log2(top * (1.0 / LEVELS)))
    codes = (values * jnp.exp2(eighths * -0.125) + WHOLE) - WHOLE
    return pack(codes), eighths


def decode(codes, eighths):
    return codes.astype(jnp.int32).astype(jnp.float32) * jnp.exp2(eighths * 0.125)


def lane_of(shape):
    return lax.broadcasted_iota(jnp.int32, shape, len(shape) - 1)


def pick_lane(values, lane):
    values = values.astype(jnp.int32).astype(jnp.float32)
    return jnp.sum(jnp.where(lane_of(values.shape) == lane, values, 0.0), axis=1, keepdims=True)


def put_lane(values, column, lane):
    return jnp.where(lane_of(values.shape) == lane, column, values)


def pack(values):
    return values.astype(jnp.int32).astype(jnp.int16)


def strip_matmul(blocks, meta, weight, count_rows, count_cols, along_rows, coded, kept, gathered, instead=None):
    builds = isinstance(weight, tuple)
    outer_tiles = count_rows if along_rows else count_cols
    width = next(w for w in (GROUP * 4, GROUP * 2, GROUP) if outer_tiles * TILE % w == 0)
    if not along_rows or isinstance(weight, tuple):
        width = min(width, GROUP * 2)
    per = width // TILE
    steps = outer_tiles // per
    inner = (count_cols if along_rows else count_rows) * TILE
    outer = outer_tiles * TILE
    tokens = sum(rows for _, rows, _ in blocks)
    first_kept = tokens - kept
    strip_shape = (width, inner) if along_rows else (inner, width)
    if builds:
        (tiles,) = weight
        kept_tiles = tiles.shape[0]
        chunk = CHUNK if kept_tiles % CHUNK == 0 else kept_tiles
        chunks = kept_tiles // chunk

    def kernel(meta, *refs):
        ins, refs = refs[: len(blocks)], refs[len(blocks) :]
        weight_ref, refs = refs[0], refs[1:]
        if instead:
            instead_ref, refs = refs[0], refs[1:]
        if coded:
            codes_ref, refs = refs[0], refs[1:]
        if kept:
            kept_ref, refs = refs[0], refs[1:]
        if gathered:
            gathered_ref, refs = refs[0], refs[1:]
        if builds:
            built_ref, refs = refs[0], refs[1:]
        held, refs = refs[0], refs[1:]
        step = pl.program_id(0)

        @pl.when(step == 0)
        def _():
            held[...] = jnp.zeros_like(held)

        def mixed(here, there):
            rows = coded // len(instead[2])
            out = []
            for (a, n), (b, m) in instead[2]:
                one, two = (v[i * rows : (i + 1) * rows] for v, i in (((here, there)[a], n), ((here, there)[b], m)))
                out.append(jnp.where(meta[instead[1]] == 1, one, two))
            return jnp.concatenate(out, axis=0)

        if builds:
            local, sems = refs

            def chunk_copy(n):
                here = pl.ds(n * chunk, chunk)
                return pltpu.make_async_copy(weight_ref.at[here], local.at[here], sems.at[n])

            @pl.when(step == 0)
            def _():
                for n in range(chunks):
                    chunk_copy(n).start()
                local[kept_tiles] = jnp.zeros((TILE, TILE), jnp.bfloat16)

            base = count_rows * count_cols
            held_chunks = (meta[base + step * per] + (chunk - 1)) // chunk
            needed = jnp.where(step == steps - 1, chunks, (meta[base + step * per + per] + (chunk - 1)) // chunk)
            lax.fori_loop(held_chunks, needed, lambda n, c: (chunk_copy(n).wait(), c)[1], 0)

            for a in range(per):
                for c in range(count_cols):
                    tile = meta[(step * per + a) * count_cols + c]
                    built_ref[a * TILE : (a + 1) * TILE, c * TILE : (c + 1) * TILE] = local[tile]
            strip = built_ref[...]
        else:
            strip = weight_ref[...]
        x = jnp.concatenate([r[...] for r in ins], axis=0) if len(ins) > 1 else ins[0][...]
        if along_rows:
            y = lax.dot_general(x, strip, (((1,), (1,)), ((), ())), preferred_element_type=jnp.float32)
        else:
            y = jnp.dot(x, strip, preferred_element_type=jnp.float32)
        if coded:
            for g in range(width // GROUP):
                codes, eighths = encode(y[:coded, g * GROUP : (g + 1) * GROUP])
                here = pl.ds(pl.multiple_of(step * width + g * GROUP, GROUP), GROUP)
                if instead:
                    codes = mixed(codes, instead_ref[:, here])
                codes_ref[:, here] = codes
                held[...] = put_lane(held[...], eighths, step * (width // GROUP) + g)

            @pl.when(step == steps - 1)
            def _():
                last = pack(held[...])
                if instead:
                    last = mixed(last, instead_ref[:, outer:])
                codes_ref[:, outer:] = last

        if kept:
            kept_ref[...] = y[first_kept:]
        if gathered:

            @pl.when(step == 0)
            def _():
                gathered_ref[...] = x

    def in_spec(rows, entry):
        def place(step, meta):
            return (0 if entry is None else meta[entry], 0)

        return pl.BlockSpec((rows, inner), place, pipeline_mode=pl.Buffered(1))

    outs, out_specs = [], []
    if coded:
        outs.append(jax.ShapeDtypeStruct((coded, outer + LANES), jnp.int16))
        out_specs.append(pl.BlockSpec((coded, outer + LANES), lambda s, m: (0, 0)))
    if kept:
        outs.append(jax.ShapeDtypeStruct((kept, outer), jnp.float32))
        out_specs.append(pl.BlockSpec((kept, width), lambda s, m: (0, s)))
    if gathered:
        outs.append(jax.ShapeDtypeStruct((tokens, inner), jnp.bfloat16))
        out_specs.append(pl.BlockSpec((tokens, inner), lambda s, m: (0, 0)))
    scratch = [pltpu.VMEM((max(coded, 8), LANES), jnp.float32)]
    strip_spec = pl.BlockSpec(strip_shape, (lambda s, m: (s, 0)) if along_rows else (lambda s, m: (0, s)))
    if builds:
        outs.append(jax.ShapeDtypeStruct((count_rows * TILE, count_cols * TILE), jnp.bfloat16))
        out_specs.append(strip_spec)
        strip_spec = pl.BlockSpec(memory_space=pl.ANY)
        scratch += [pltpu.VMEM((kept_tiles + 1, TILE, TILE), jnp.bfloat16), pltpu.SemaphoreType.DMA((chunks,))]
    return pl.pallas_call(
        kernel,
        out_shape=outs,
        grid_spec=pltpu.PrefetchScalarGridSpec(
            num_scalar_prefetch=1,
            grid=(steps,),
            in_specs=[in_spec(rows, entry) for _, rows, entry in blocks]
            + [strip_spec]
            + ([pl.BlockSpec((coded, outer + LANES), lambda s, m: (0, 0), pipeline_mode=pl.Buffered(1))] * bool(instead)),
            out_specs=out_specs,
            scratch_shapes=scratch,
        ),
        compiler_params=params(),
        cost_estimate=pl.CostEstimate(
            flops=2 * tokens * inner * outer,
            bytes_accessed=inner * outer * 2 + tokens * (inner * 2 + outer * 4),
            transcendentals=0,
        ),
        name="dgrad" if along_rows else "forward",
    )(meta, *[a for a, _, _ in blocks], tiles if builds else weight, *([instead[0]] if instead else []))


def tile_products(lefts, rights, meta, kept_tiles, count_rows, count_cols, factor, part, before):
    tokens = sum(rows * len(entries) for _, rows, entries in lefts)
    first, count = part
    wide_rows, wide_cols = count * TILE, count_cols * TILE
    per = next(p for p in (8, 4, 2, 1) if count % p == 0)
    steps = count // per
    spots = count_rows * count_cols

    def kernel(meta, *refs):
        left_refs, refs = refs[: len(lefts)], refs[len(lefts) :]
        right_refs, refs = refs[: len(rights)], refs[len(rights) :]
        if before is not None:
            refs = refs[1:]
        out_ref, left_all, right_all, turned, found, left_sems, right_sems, out_sems = refs
        i = pl.program_id(0)

        def copies(group, group_refs, whole, sems, from_col, to_col, width):
            n = 0
            for (_, rows, entries), ref in zip(group, group_refs):
                for b, entry in enumerate(entries):
                    to = pl.multiple_of(meta[entry] * rows, rows)
                    yield pltpu.make_async_copy(
                        ref.at[pl.ds(b * rows, rows), pl.ds(from_col, width)],
                        whole.at[pl.ds(to, rows), pl.ds(to_col, width)],
                        sems.at[n],
                    )
                    n += 1

        def left_copies(step):
            at = step * per * TILE
            return copies(lefts, left_refs, left_all, left_sems.at[step], first * TILE + at, at, per * TILE)

        def right_copies():
            return copies(rights, right_refs, right_all, right_sems, 0, 0, wide_cols)

        @pl.when(i == 0)
        def _():
            for c in left_copies(0):
                c.start()
            for c in right_copies():
                c.start()
            for n in range(1, steps):
                for c in left_copies(n):
                    c.start()
            for c in left_copies(0):
                c.wait()
            turned[0] = left_all[:, : per * TILE].T
            for n in range(1, steps):
                for c in left_copies(n):
                    c.wait()
            for c in right_copies():
                c.wait()

        now = lax.rem(i, 2)
        for b in range(0, count_cols, 4):
            n = min(4, count_cols - b)
            sums = jnp.dot(
                turned[now], right_all[:, b * TILE : (b + n) * TILE], preferred_element_type=jnp.float32
            )
            for a in range(per):
                for e in range(n):
                    tile = meta[(first + i * per + a) * count_cols + b + e]
                    found[tile] = sums[a * TILE : (a + 1) * TILE, e * TILE : (e + 1) * TILE] * factor
        for a in range(per if steps > 1 else 0):
            ahead = jnp.minimum(i + 1, steps - 1) * per + a
            turned[1 - now, a * TILE : (a + 1) * TILE, :] = left_all[
                :, pl.ds(pl.multiple_of(ahead * TILE, TILE), TILE)
            ].T

        def out_copies(low, high, begin):
            many = (high - low) // OUT_CHUNK

            def copy(at, size, sem):
                c = pltpu.make_async_copy(found.at[pl.ds(at, size)], out_ref.at[pl.ds(at, size)], sem)
                c.start() if begin else c.wait()

            def chunk(n, c):
                copy(low + n * OUT_CHUNK, OUT_CHUNK, out_sems.at[0])
                return c

            def single(n, c):
                copy(n, 1, out_sems.at[1])
                return c

            lax.fori_loop(0, many, chunk, 0)
            lax.fori_loop(low + many * OUT_CHUNK, high, single, 0)

        def bounds(n):
            row = spots + first + n * per
            return meta[row], meta[row + per]

        out_copies(*bounds(i), True)

        @pl.when(i == steps - 1)
        def _():
            for n in range(steps):
                out_copies(*bounds(n), False)

    operands = [a for a, _, _ in lefts] + [a for a, _, _ in rights]
    aliases = {}
    if before is not None:
        aliases = {1 + len(operands): 0}
        operands.append(before)
    return pl.pallas_call(
        kernel,
        out_shape=jax.ShapeDtypeStruct((kept_tiles, TILE, TILE), jnp.float32),
        grid_spec=pltpu.PrefetchScalarGridSpec(
            num_scalar_prefetch=1,
            grid=(steps,),
            in_specs=[pl.BlockSpec(memory_space=pl.ANY)] * len(operands),
            out_specs=pl.BlockSpec(memory_space=pl.ANY),
            scratch_shapes=[
                pltpu.VMEM((tokens, wide_rows), jnp.bfloat16),
                pltpu.VMEM((tokens, wide_cols), jnp.bfloat16),
                pltpu.VMEM((2, per * TILE, tokens), jnp.bfloat16),
                pltpu.VMEM((kept_tiles + 1, TILE, TILE), jnp.float32),
                pltpu.SemaphoreType.DMA((steps, sum(len(e) for _, _, e in lefts))),
                pltpu.SemaphoreType.DMA((sum(len(e) for _, _, e in rights),)),
                pltpu.SemaphoreType.DMA((2,)),
            ],
        ),
        input_output_aliases=aliases,
        compiler_params=params(),
        cost_estimate=pl.CostEstimate(
            flops=2 * tokens * wide_rows * wide_cols,
            bytes_accessed=tokens * (wide_rows + wide_cols) * 2
            + kept_tiles * TILE * TILE * 4 * count // count_rows,
            transcendentals=0,
        ),
        name="wgrad",
    )(meta, *operands)


def add_received(locals_, received, sums, meta, rows, wide, sends, keep, keep_type):
    span = 1024 if wide % 1024 == 0 else wide
    steps, groups = wide // span, span // GROUP

    def kernel(meta, *refs):
        local_refs, refs = refs[: len(locals_)], refs[len(locals_) :]
        code_refs, refs = refs[: 2 * len(received)], refs[2 * len(received) :]
        send_refs, (keep_ref, held) = refs[: len(sends)], refs[len(sends) :]
        step = pl.program_id(0)

        @pl.when(step == 0)
        def _():
            held[...] = jnp.zeros_like(held)

        for g in range(groups):
            here = slice(g * GROUP, (g + 1) * GROUP)
            there = pl.ds(pl.multiple_of(step * span + g * GROUP, GROUP), GROUP)
            totals = []
            for local, others in sums:
                total = local_refs[local][:, here]
                for n in others:
                    eighths = pick_lane(code_refs[2 * n + 1][...], step * groups + g)
                    total = total + decode(code_refs[2 * n][:, here], eighths)
                totals.append(total)
            keep_ref[:, here] = keep(totals, meta).astype(keep_type)
            for n, send in enumerate(sends):
                codes, eighths = encode(send(totals, meta))
                send_refs[n][:, there] = codes
                held[n] = put_lane(held[n], eighths, step * groups + g)

        @pl.when(step == steps - 1)
        def _():
            for n in range(len(sends)):
                send_refs[n][:, wide:] = pack(held[n])

    in_specs = [pl.BlockSpec((rows, span), lambda s, m, e=e: (m[e], s)) for _, e in locals_]
    operands = [v for v, _ in locals_]
    for codes, entry in received:
        in_specs += [
            pl.BlockSpec((rows, span), lambda s, m, e=entry: (m[e], s)),
            pl.BlockSpec((rows, LANES), lambda s, m, e=entry: (m[e], wide // LANES)),
        ]
        operands += [codes, codes]
    outs = [jax.ShapeDtypeStruct((rows, wide + LANES), jnp.int16)] * len(sends)
    out_specs = [pl.BlockSpec((rows, wide + LANES), lambda s, m: (0, 0))] * len(sends)
    outs.append(jax.ShapeDtypeStruct((rows, wide), keep_type))
    out_specs.append(pl.BlockSpec((rows, span), lambda s, m: (0, s)))
    return pl.pallas_call(
        kernel,
        out_shape=outs,
        grid_spec=pltpu.PrefetchScalarGridSpec(
            num_scalar_prefetch=1,
            grid=(steps,),
            in_specs=in_specs,
            out_specs=out_specs,
            scratch_shapes=[pltpu.VMEM((max(len(sends), 1), rows, LANES), jnp.float32)],
        ),
        compiler_params=params(),
        cost_estimate=pl.CostEstimate(
            flops=8 * rows * wide, bytes_accessed=len(operands) * rows * wide * 3, transcendentals=0
        ),
        name="add_received",
    )(meta, *operands)


def tile_places(tile_rows, tile_cols, count_rows, count_cols):
    kept = tile_rows.shape[0]
    position = tile_rows * count_cols + tile_cols
    short = jnp.arange(kept, dtype=jnp.int32) - kept
    spot = jnp.arange(count_rows * count_cols, dtype=jnp.int32)
    places = jnp.sum(jnp.where(position[None, :] == spot[:, None], short[None, :], 0), axis=1) + kept
    rows = jnp.arange(count_rows, dtype=jnp.int32)
    ends = jnp.sum((tile_rows[None, :] <= rows[:, None]).astype(jnp.int32), axis=1)
    return places, ends


def tables(tile_rows, tile_cols, count_rows, count_cols, extras):
    places, ends = tile_places(tile_rows, tile_cols, count_rows, count_cols)
    return jnp.concatenate([places, jnp.zeros((1,), jnp.int32), ends, extras])


def shards_general(activations, weight_tiles, tile_rows, tile_cols, grad_out):
    tiles = weight_tiles[0, 0]
    count_rows = activations.shape[2] // TILE
    count_cols = grad_out.shape[2] // TILE
    meta = tables(tile_rows[0, 0], tile_cols[0, 0], count_rows, count_cols, jnp.zeros((1,), jnp.int32))
    zero = count_rows * count_cols + 1 + count_rows
    act = lax.all_gather(activations[0], "col", axis=0, tiled=True)
    grad = lax.all_gather(grad_out[0], "row", axis=0, tiled=True)
    tokens = act.shape[0]
    back, weight = strip_matmul([(grad, tokens, None)], meta, (tiles,), count_rows, count_cols, True, 0, tokens, False)
    (partial,) = strip_matmul([(act, tokens, None)], meta, weight, count_rows, count_cols, False, 0, tokens, False)
    output = lax.psum_scatter(partial, "row", scatter_dimension=0, tiled=True).astype(jnp.bfloat16)[None]
    grad_input = lax.psum_scatter(back, "col", scatter_dimension=0, tiled=True).astype(jnp.bfloat16)[None]
    groups = lax.axis_size("depth")
    all_act = lax.all_gather(act, "depth", axis=0, tiled=True)
    all_grad = lax.all_gather(grad, "depth", axis=0, tiled=True)
    grad_tiles = tile_products(
        [(all_act, tokens * groups, [zero])],
        [(all_grad, tokens * groups, [zero])],
        meta,
        tiles.shape[0],
        count_rows,
        count_cols,
        1.0 / math.sqrt(tokens * groups),
        (0, count_rows),
        None,
    )
    return output, grad_input, grad_tiles[None, None]


FIRST_SET, SECOND_SET = (0, 1, 2, 6), (3, 4, 5, 7)


def block_pairs():
    spot = {k: (1, n) for n, k in enumerate(FIRST_SET)} | {k: (0, n) for n, k in enumerate(SECOND_SET)}
    return [(spot[n], spot[n + 4]) for n in range(4)]


def pair_entries(row, col, size, groups):
    y, z0, z1 = col % 2, col // 2 % 2, col // 4
    keep = [p[z1 != row] for p in (block_pairs()[n ^ (col % 4)] for n in range(4))]
    return {
        "dgrad": [1 - y, 3 - y, y, 2 + y],
        "near": [int(z1 != row)],
        "z0": [z0, 1 - z0],
        "mine": [int(z1 == row)],
        "const": [0, 1],
        "left": [g * size + (col ^ k) for g in range(groups) for k in FIRST_SET + SECOND_SET],
        "right": [2 * g + r for g in range(groups) for r in (row, 1 - row)],
        "codes": [n ^ (col % 4) for n in range(4)],
        "second": [1 - k[0] for k in keep],
        "in_first": [k[1] * k[0] for k in keep],
        "in_second": [k[1] * (1 - k[0]) for k in keep],
    }


def swap(value, axis, bit, size):
    return lax.ppermute(value, axis, [(i, i ^ bit) for i in range(size)])


def shards_paired(activations, weight_tiles, tile_rows, tile_cols, grad_out):
    tiles = weight_tiles[0, 0]
    count_rows = activations.shape[2] // TILE
    count_cols = grad_out.shape[2] // TILE
    wide_rows = activations.shape[2]
    size = lax.axis_size("col")
    groups = lax.axis_size("depth")
    row, col = lax.axis_index("row"), lax.axis_index("col")
    block = activations.shape[1]
    half = grad_out.shape[1]
    values = [[sum(pair_entries(r, c, size, groups).values(), []) for c in range(size)] for r in range(2)]
    extras = lax.dynamic_slice(
        jnp.asarray(np.array(values, np.int32)), (row, col, 0), (1, 1, len(values[0][0]))
    ).reshape(-1)
    meta = tables(tile_rows[0, 0], tile_cols[0, 0], count_rows, count_cols, extras)
    at, n = {}, count_rows * count_cols + 1 + count_rows
    for name, entries in pair_entries(0, 0, size, groups).items():
        at[name] = n
        n += len(entries)

    def swap_col(value, bit):
        return swap(value, "col", bit, size)

    def swap_depth(value):
        return swap(value, "depth", 1, 2)

    def swap_row(value):
        return swap(value, "row", 1, 2)

    grad_mine = grad_out[0]
    own = activations[0]
    grad_other = swap_row(grad_mine)
    b2 = swap_col(own, 2)
    b6 = swap_col(own, 6)
    b1 = swap_col(own, 1)
    b3 = swap_col(b1, 2)
    b4 = swap_col(b6, 2)
    b7 = swap_col(b6, 1)
    b5 = swap_col(b7, 2)

    def dgrad(grad, weight):
        blocks = [(grad, block, at["dgrad"] + e) for e in range(4)]
        return strip_matmul(blocks, meta, weight, count_rows, count_cols, True, 2 * block, 2 * block, False)

    def forward(blocks, weight, instead):
        blocks = [(b, block, None) for b in blocks]
        return strip_matmul(blocks, meta, weight, count_rows, count_cols, False, half, half, True, instead)

    codes_mine, kept_mine, weight = dgrad(grad_mine, (tiles,))
    codes_mine = swap_col(codes_mine, 1)
    first_codes, first_kept, first_act = forward([own, b1, b2, b6], weight, None)
    codes_other, kept_other = dgrad(grad_other, weight)
    codes_other = swap_col(codes_other, 1)
    out_codes, second_kept, second_act = forward([b3, b4, b5, b7], weight, (first_codes, at["near"], block_pairs()))
    out_codes = swap_row(out_codes)

    z0, const, mine = at["z0"], at["const"], at["mine"]

    def choose(yes, no):
        return lambda s, m: jnp.where(m[mine] == 1, s[yes], s[no])

    *codes, kept = add_received(
        [(v, z0 + e) for v in (kept_mine, kept_other) for e in (0, 1)],
        [(v, z0 + e) for v in (codes_mine, codes_other) for e in (0, 1)],
        [(n, [n]) for n in range(4)],
        meta,
        block,
        wide_rows,
        [choose(1, 3), choose(2, 0), choose(3, 1)],
        choose(0, 2),
        jnp.float32,
    )
    codes = [swap_col(v, 2 * n + 2) for n, v in enumerate(codes)]

    partner = [swap_depth(v) for v in (first_act, second_act, grad_mine, grad_other)]
    lefts = [
        (v, block, [at["left"] + 4 * n + k for k in range(4)])
        for n, v in enumerate((first_act, second_act, *partner[:2]))
    ]
    rights = [(v, half, [at["right"] + n]) for n, v in enumerate((grad_mine, grad_other, *partner[2:]))]

    def wgrad(part, before):
        return tile_products(
            lefts,
            rights,
            meta,
            tiles.shape[0],
            count_rows,
            count_cols,
            1.0 / math.sqrt(size * block * groups),
            part,
            before,
        )

    grad_tiles = wgrad((0, count_rows), None)
    (grad_input,) = add_received(
        [(kept, const)],
        [(v, const) for v in codes],
        [(0, [0, 1, 2])],
        meta,
        block,
        wide_rows,
        [],
        lambda s, m: s[0],
        jnp.bfloat16,
    )
    output = join_output(first_kept, second_kept, out_codes, meta, at, block)
    return output[None], grad_input[None], grad_tiles[None, None]


def join_output(first, second, codes, meta, at, rows):
    wide = first.shape[1]
    blocks = first.shape[0] // rows

    def kernel(meta, first_ref, second_ref, codes_ref, out_ref):
        use_second = meta[at["second"] + pl.program_id(0)] == 1
        for g in range(wide // GROUP):
            here = slice(g * GROUP, (g + 1) * GROUP)
            local = jnp.where(use_second, second_ref[:, here], first_ref[:, here])
            eighths = pick_lane(codes_ref[:, wide:], g)
            out_ref[:, here] = (local + decode(codes_ref[:, here], eighths)).astype(jnp.bfloat16)

    return pl.pallas_call(
        kernel,
        out_shape=jax.ShapeDtypeStruct((blocks * rows, wide), jnp.bfloat16),
        grid_spec=pltpu.PrefetchScalarGridSpec(
            num_scalar_prefetch=1,
            grid=(blocks,),
            in_specs=[
                pl.BlockSpec((rows, wide), lambda n, m: (m[at["in_first"] + n], 0)),
                pl.BlockSpec((rows, wide), lambda n, m: (m[at["in_second"] + n], 0)),
                pl.BlockSpec((rows, wide + LANES), lambda n, m: (m[at["codes"] + n], 0)),
            ],
            out_specs=pl.BlockSpec((rows, wide), lambda n, m: (n, 0)),
        ),
        compiler_params=params(),
        cost_estimate=pl.CostEstimate(flops=8 * first.size, bytes_accessed=first.size * 8, transcendentals=0),
        name="join_output",
    )(meta, first, second, codes)


def solution(mesh):
    specs = (
        P("depth", "col", "row"),
        P("row", "col", None, None, None),
        P("row", "col", None),
        P("row", "col", None),
        P("depth", "row", "col"),
    )
    paired = mesh.shape["row"] == 2 and mesh.shape["col"] == 8 and mesh.shape["depth"] == 2

    def body(*args):
        return (shards_paired if paired else shards_general)(*args)

    return jax.shard_map(
        body,
        mesh=mesh,
        in_specs=specs,
        out_specs=(specs[4], specs[0], specs[1]),
        check_vma=False,
    )
```

time: 253 us -> 216 us (0.85)
  Pallas kernels: 153 us -> 134 us
  waiting for transfers between devices: 62.7 us -> 56.1 us
  starting transfers between devices: 27.1 us -> 20.8 us
  local copies, waits for them, and re-layouts: 5.38 us -> 0.7 us
    pallas_call x2 -> x1, Pallas kernels: 57.2 us -> 42.4 us  [tile_products(): pl.pallas_call(kernel, out_shape=jax.ShapeDtypeStruct((kept_tiles, TILE,...]
    ppermute x17 -> x18, waiting for transfers between devices: 62.7 us -> 56.1 us  [swap(): return lax.ppermute(value, axis, [(i, i ^ bit) for i in range(size)])]
    ppermute x17 -> x18, starting transfers between devices: 27.1 us -> 20.8 us  [swap(): return lax.ppermute(value, axis, [(i, i ^ bit) for i in range(size)])]
    pallas_call x3 -> x2, Pallas kernels: 15.9 us -> 11.6 us  [add_received(): pl.pallas_call(kernel, out_shape=outs, grid_spec=pltpu.PrefetchScalarGrid...]
    unnamed x22 -> x4, local copies, waits for them, and re-layouts: 3.34 us -> 0.01 us
  transfers between devices with their start and end apart: 17 -> 18, of which waited for: 5 -> 5; matrix products, arithmetic and copies ran while one was open for 2% -> 1% of each run, Pallas kernels for 57% -> 43%
where the time goes in v2:
time: 216 us; the launch traced here: 215 us
  Pallas kernels  134 us (62%)
  waiting for transfers between devices  56.1 us (26%)
  starting transfers between devices  20.8 us (10%)
  other arithmetic  2.41 us (1%)
    pallas_call x4, Pallas kernels, strip_matmul(): pl.pallas_call(kernel, out_shape=outs, grid_spec=pltpu.PrefetchScalarGrid...  73.8 us
    ppermute x18, waiting for transfers between devices, swap(): return lax.ppermute(value, axis, [(i, i ^ bit) for i in range(size)])  56.1 us
    pallas_call x1, Pallas kernels, tile_products(): pl.pallas_call(kernel, out_shape=jax.ShapeDtypeStruct((kept_tiles, TILE,...  42.4 us
    ppermute x18, starting transfers between devices, swap(): return lax.ppermute(value, axis, [(i, i ^ bit) for i in range(size)])  20.8 us
    pallas_call x2, Pallas kernels, add_received(): pl.pallas_call(kernel, out_shape=outs, grid_spec=pltpu.PrefetchScalarGrid...  11.6 us
    pallas_call x1, Pallas kernels, join_output(): pl.pallas_call(kernel, out_shape=jax.ShapeDtypeStruct((blocks * rows, wid...  5.84 us
  transfers between devices with their start and end apart: 18, of which 5 were waited for; matrix products, arithmetic and copies ran while one was open for 1% of the time, Pallas kernels for 43%

profile of v2, /device:TPU:0, one launch (start us, length us, event | category | flops | bytes accessed | tf_op | source)
XLA Modules:
  0.0 214.6 jit_solution(17280493447513151136)
XLA Ops:
  0.6 3.0 %collective-permute-start.8 = (bf16[256,3584]{1,0:T(8,128)(2,1)}, bf16[256,3584]{1,0:T(8,128)(2,1)}, u32[]{:S(2)}, u32[]{:S(2)}) collective-permute-start(bf16[256,3584]{1,0:T(8,128)(2,1)} %bitcast.20), channel_id=1, source_target_pairs={{0,16},{16,0},{1,17},{17,1},{2,18},{18,2},{3,19},{19,3},{4,20},{20... | collective-permute-start | bytes 5505032 | tf_op jit(solution)/shard_map/ppermute | solution.py:472
  3.7 1.5 collective-permute-start
  5.2 1.6 collective-permute-start.1
  6.8 2.5 %collective-permute-start.2 = (bf16[64,4096]{1,0:T(8,128)(2,1)}, bf16[64,4096]{1,0:T(8,128)(2,1)}, u32[]{:S(2)}, u32[]{:S(2)}) collective-permute-start(bf16[64,4096]{1,0:T(8,128)(2,1)} %bitcast.13), channel_id=1, source_target_pairs={{0,12},{2,14},{4,8},{6,10},{8,4},{10,6},{12,0},{14,2},{1,13},{3,15... | collective-permute-start | bytes 1572872 | tf_op jit(solution)/shard_map/ppermute | solution.py:472
  9.9 0.8 convert_reduce_fusion
  12.3 19.1 %dgrad.2 = (s16[128,4224]{1,0:T(8,128)(2,1)}, f32[128,4096]{1,0:T(8,128)}, bf16[4096,3584]{1,0:T(8,128)(2,1)}) custom-call(s32[975]{0:T(1024)} %pad_add_fusion.meta, bf16[256,3584]{1,0:T(8,128)(2,1)} %bitcast.21, bf16[256,3584]{1,0:T(8,128)(2,1)} %bitcast.22, bf16[256,3584]{1,0:T(8,128)(2,1)} %bitcast.23, bf16[256,3584]{1,0:T(8,128)(2,1)} %bitcast.24, ...), custom_call_target="tpu_custom_call" | custom-call | flops 7516192768 | bytes 35389440 | tf_op jit(solution)/shard_map/dgrad/pallas_call | solution.py:179
  32.0 1.5 collective-permute-start.5
  33.6 10.4 %collective-permute-done.8.refs_0_.refs_1_.refs_2_.refs_3_.refs_5_ = bf16[256,3584]{1,0:T(8,128)(2,1)} collective-permute-done((bf16[256,3584]{1,0:T(8,128)(2,1)}, bf16[256,3584]{1,0:T(8,128)(2,1)}, u32[]{:S(2)}, u32[]{:S(2)}) %collective-permute-start.8) | collective-permute-done | bytes 1835040 | tf_op jit(solution)/shard_map/ppermute | solution.py:472
  44.0 15.8 %dgrad.3 = (s16[128,4224]{1,0:T(8,128)(2,1)}, f32[128,4096]{1,0:T(8,128)}) custom-call(s32[975]{0:T(1024)} %pad_add_fusion.meta, bf16[256,3584]{1,0:T(8,128)(2,1)} %collective-permute-done.8.refs_0_.refs_1_.refs_2_.refs_3_.refs_5_, bf16[256,3584]{1,0:T(8,128)(2,1)} %collective-permute-done.8.refs_0_.refs_1_.refs_2_.refs_3_.refs_5_, ...), custom_call_target="tpu_custom_call" | custom-call | flops 7516192768 | bytes 35389440 | tf_op jit(solution)/shard_map/dgrad/pallas_call | solution.py:179
  59.8 1.8 collective-permute-start.10
  61.5 1.6 collective-permute-start.4
  63.6 6.2 %collective-permute-done.5.refs_3_ = bf16[64,4096]{1,0:T(8,128)(2,1)} collective-permute-done((bf16[64,4096]{1,0:T(8,128)(2,1)}, bf16[64,4096]{1,0:T(8,128)(2,1)}, u32[]{:S(2)}, u32[]{:S(2)}) %collective-permute-start.5) | collective-permute-done | bytes 524320 | tf_op jit(solution)/shard_map/ppermute | solution.py:472
  70.5 19.1 %forward.2 = (s16[256,3712]{1,0:T(8,128)(2,1)}, f32[256,3584]{1,0:T(8,128)}, bf16[256,4096]{1,0:T(8,128)(2,1)}) custom-call(s32[975]{0:T(1024)} %pad_add_fusion.meta, bf16[64,4096]{1,0:T(8,128)(2,1)} %bitcast.14, bf16[64,4096]{1,0:T(8,128)(2,1)} %collective-permute-done.refs_1_, bf16[64,4096]{1,0:T(8,128)(2,1)} %copy-done.1, ...), custom_call_target="tpu_custom_call" | custom-call | flops 7516192768 | bytes 35127296 | tf_op jit(solution)/shard_map/forward/pallas_call | solution.py:179
  89.7 1.1 collective-permute-done.10.refs_8_.refs_9_.refs_10_.refs_11_
  90.7 6.9 %add_received.2 = (s16[64,4224]{1,0:T(8,128)(2,1)}, s16[64,4224]{1,0:T(8,128)(2,1)}, s16[64,4224]{1,0:T(8,128)(2,1)}, f32[64,4096]{1,0:T(8,128)}) custom-call(s32[975]{0:T(1024)} %pad_add_fusion.meta, f32[128,4096]{1,0:T(8,128)} %get-tuple-element.23.refs_0_.refs_1_, f32[128,4096]{1,0:T(8,128)} %get-tuple-element.23.refs_0_.refs_1_, ...), custom_call_target="tpu_custom_call" | custom-call | flops 2097152 | bytes 9437184 | tf_op jit(solution)/shard_map/add_received/pallas_call | solution.py:381
  97.7 0.7 collective-permute-start.11
  98.4 1.2 collective-permute-start.12
  99.7 2.5 %collective-permute-start.13 = (s16[64,4224]{1,0:T(8,128)(2,1)}, s16[64,4224]{1,0:T(8,128)(2,1)}, u32[]{:S(2)}, u32[]{:S(2)}) collective-permute-start(s16[64,4224]{1,0:T(8,128)(2,1)} %get-tuple-element.30), channel_id=1, source_target_pairs={{0,12},{2,14},{4,8},{6,10},{8,4},{10,6},{12,0},{14,2},{1,13},{3,15... | collective-permute-start | bytes 1622024 | tf_op jit(solution)/shard_map/ppermute | solution.py:472
  102.1 19.9 %forward.3 = (s16[256,3712]{1,0:T(8,128)(2,1)}, f32[256,3584]{1,0:T(8,128)}, bf16[256,4096]{1,0:T(8,128)(2,1)}) custom-call(s32[975]{0:T(1024)} %pad_add_fusion.meta, bf16[64,4096]{1,0:T(8,128)(2,1)} %collective-permute-done.3.refs_0_, bf16[64,4096]{1,0:T(8,128)(2,1)} %collective-permute-done.4.refs_1_, bf16[64,4096]{1,0:T(8,128)(2,1)} %collective-permute-done.6.refs_2_, ...), custom_call_target="tpu_custom_call" | custom-call | flops 7516192768 | bytes 35127296 | tf_op jit(solution)/shard_map/forward/pallas_call | solution.py:179
  122.6 15.3 %collective-permute-done.12.refs_3_.refs_4_ = s16[64,4224]{1,0:T(8,128)(2,1)} collective-permute-done((s16[64,4224]{1,0:T(8,128)(2,1)}, s16[64,4224]{1,0:T(8,128)(2,1)}, u32[]{:S(2)}, u32[]{:S(2)}) %collective-permute-start.12) | collective-permute-done | bytes 540704 | tf_op jit(solution)/shard_map/ppermute | solution.py:472
  138.5 4.7 %add_received.3 = bf16[64,4096]{1,0:T(8,128)(2,1)} custom-call(s32[975]{0:T(1024)} %pad_add_fusion.meta, f32[64,4096]{1,0:T(8,128)} %get-tuple-element.27.refs_0_, s16[64,4224]{1,0:T(8,128)(2,1)} %copy-done, s16[64,4224]{1,0:T(8,128)(2,1)} %copy-done, s16[64,4224]{1,0:T(8,128)(2,1)} %collective-permute-done.12.refs_3_.refs_4_, ...), custom_call_target="tpu_custom_call" | custom-call | flops 2097152 | bytes 5505024 | tf_op jit(solution)/shard_map/add_received/pallas_call | solution.py:381
  143.2 23.0 %collective-permute-done.7.codes_ref = s16[256,3712]{1,0:T(8,128)(2,1)} collective-permute-done((s16[256,3712]{1,0:T(8,128)(2,1)}, s16[256,3712]{1,0:T(8,128)(2,1)}, u32[]{:S(2)}, u32[]{:S(2)}) %collective-permute-start.7) | collective-permute-done | bytes 1900576 | tf_op jit(solution)/shard_map/ppermute | solution.py:472
  166.1 5.8 %join_output.1 = bf16[256,3584]{1,0:T(8,128)(2,1)} custom-call(s32[975]{0:T(1024)} %pad_add_fusion.meta, f32[256,3584]{1,0:T(8,128)} %get-tuple-element.19.first_ref, f32[256,3584]{1,0:T(8,128)} %get-tuple-element.21.second_ref, s16[256,3712]{1,0:T(8,128)(2,1)} %collective-permute-done.7.codes_ref), custom_call_target="tpu_custom_call" | custom-call | flops 7340032 | bytes 7340032 | tf_op jit(solution)/shard_map/join_output/pallas_call | solution.py:597
  172.0 42.4 %wgrad.1 = f32[448,128,128]{2,1,0:T(8,128)} custom-call(s32[975]{0:T(1024)} %pad_add_fusion.meta, bf16[256,4096]{1,0:T(8,128)(2,1)} %get-tuple-element.31.refs_0_, bf16[256,4096]{1,0:T(8,128)(2,1)} %get-tuple-element.32.refs_1_, bf16[256,4096]{1,0:T(8,128)(2,1)} %collective-permute-done.14.refs_2_, bf16[256,4096]{1,0:T(8,128)(2,1)} %collective-permute-done.15.refs_3_, ...), custom_call_target="tpu_custom_call" | custom-call | flops 30064771072 | bytes 45088768 | tf_op jit(solution)/shard_map/wgrad/pallas_call | solution.py:304
  (30 shorter events, 5.2 us)
Async XLA Ops:
  0.6 43.4 %collective-permute-start.8 = (bf16[256,3584]{1,0:T(8,128)(2,1)}, bf16[256,3584]{1,0:T(8,128)(2,1)}, u32[]{:S(2)}, u32[]{:S(2)}) collective-permute-start(bf16[256,3584]{1,0:T(8,128)(2,1)} %bitcast.20), channel_id=1, source_target_pairs={{0,16},{16,0},{1,17},{17,1},{2,18},{18,2},{3,19},{19,3},{4,20},{20... | collective-permute-start | bytes 5505032 | tf_op jit(solution)/shard_map/ppermute | solution.py:472
  3.7 57.9 %collective-permute-start = (bf16[64,4096]{1,0:T(8,128)(2,1)}, bf16[64,4096]{1,0:T(8,128)(2,1)}, u32[]{:S(2)}, u32[]{:S(2)}) collective-permute-start(bf16[64,4096]{1,0:T(8,128)(2,1)} %bitcast.11), channel_id=1, source_target_pairs={{0,2},{2,0},{4,6},{6,4},{8,10},{10,8},{12,14},{14,12},{1,3},{3,1},... | collective-permute-start | bytes 1572872 | tf_op jit(solution)/shard_map/ppermute | solution.py:472
  5.2 57.9 %collective-permute-start.1 = (bf16[64,4096]{1,0:T(8,128)(2,1)}, bf16[64,4096]{1,0:T(8,128)(2,1)S(1)}, u32[]{:S(2)}, u32[]{:S(2)}) collective-permute-start(bf16[64,4096]{1,0:T(8,128)(2,1)} %bitcast.12), channel_id=1, source_target_pairs={{0,4},{2,6},{4,0},{6,2},{8,12},{10,14},{12,8},{14,10},{1,5},{3,7},... | collective-permute-start | bytes 1572872 | tf_op jit(solution)/shard_map/ppermute | solution.py:472
  6.8 25.3 %collective-permute-start.2 = (bf16[64,4096]{1,0:T(8,128)(2,1)}, bf16[64,4096]{1,0:T(8,128)(2,1)}, u32[]{:S(2)}, u32[]{:S(2)}) collective-permute-start(bf16[64,4096]{1,0:T(8,128)(2,1)} %bitcast.13), channel_id=1, source_target_pairs={{0,12},{2,14},{4,8},{6,10},{8,4},{10,6},{12,0},{14,2},{1,13},{3,15... | collective-permute-start | bytes 1572872 | tf_op jit(solution)/shard_map/ppermute | solution.py:472
  31.5 58.1 %collective-permute-start.9 = (s16[128,4224]{1,0:T(8,128)(2,1)}, s16[128,4224]{1,0:T(8,128)(2,1)}, u32[]{:S(2)}, u32[]{:S(2)}) collective-permute-start(s16[128,4224]{1,0:T(8,128)(2,1)} %get-tuple-element.25), channel_id=1, source_target_pairs={{0,2},{2,0},{4,6},{6,4},{8,10},{10,8},{12,14},{14,12},{1,3},{3,1},... | collective-permute-start | bytes 3244040 | tf_op jit(solution)/shard_map/ppermute | solution.py:472
  32.0 37.8 %collective-permute-start.5 = (bf16[64,4096]{1,0:T(8,128)(2,1)}, bf16[64,4096]{1,0:T(8,128)(2,1)}, u32[]{:S(2)}, u32[]{:S(2)}) collective-permute-start(bf16[64,4096]{1,0:T(8,128)(2,1)} %collective-permute-done.2.refs_3_), channel_id=1, source_target_pairs={{0,2},{2,0},{4,6},{6,4},{8,10},{10,8},{12,14},{14,12},{1,3},{3,1},... | collective-permute-start | bytes 1572872 | tf_op jit(solution)/shard_map/ppermute | solution.py:472
  59.8 31.0 %collective-permute-start.10 = (s16[128,4224]{1,0:T(8,128)(2,1)}, s16[128,4224]{1,0:T(8,128)(2,1)}, u32[]{:S(2)}, u32[]{:S(2)}) collective-permute-start(s16[128,4224]{1,0:T(8,128)(2,1)} %get-tuple-element.26), channel_id=1, source_target_pairs={{0,2},{2,0},{4,6},{6,4},{8,10},{10,8},{12,14},{14,12},{1,3},{3,1},... | collective-permute-start | bytes 3244040 | tf_op jit(solution)/shard_map/ppermute | solution.py:472
  61.5 38.1 %collective-permute-start.4 = (bf16[64,4096]{1,0:T(8,128)(2,1)}, bf16[64,4096]{1,0:T(8,128)(2,1)}, u32[]{:S(2)}, u32[]{:S(2)}) collective-permute-start(bf16[64,4096]{1,0:T(8,128)(2,1)} %collective-permute-done.2.refs_3_), channel_id=1, source_target_pairs={{0,4},{2,6},{4,0},{6,2},{8,12},{10,14},{12,8},{14,10},{1,5},{3,7},... | collective-permute-start | bytes 1572872 | tf_op jit(solution)/shard_map/ppermute | solution.py:472
  63.1 7.4 %copy-start.1 = (bf16[64,4096]{1,0:T(8,128)(2,1)}, bf16[64,4096]{1,0:T(8,128)(2,1)S(1)}, u32[]{:S(2)}) copy-start(bf16[64,4096]{1,0:T(8,128)(2,1)S(1)} %collective-permute-done.1.refs_2_) | copy-start | bytes 1572868
  63.1 35.3 %collective-permute-start.3 = (bf16[64,4096]{1,0:T(8,128)(2,1)}, bf16[64,4096]{1,0:T(8,128)(2,1)}, u32[]{:S(2)}, u32[]{:S(2)}) collective-permute-start(bf16[64,4096]{1,0:T(8,128)(2,1)} %collective-permute-done.refs_1_), channel_id=1, source_target_pairs={{0,4},{2,6},{4,0},{6,2},{8,12},{10,14},{12,8},{14,10},{1,5},{3,7},... | collective-permute-start | bytes 1572872 | tf_op jit(solution)/shard_map/ppermute | solution.py:472
  69.8 32.3 %collective-permute-start.6 = (bf16[64,4096]{1,0:T(8,128)(2,1)}, bf16[64,4096]{1,0:T(8,128)(2,1)}, u32[]{:S(2)}, u32[]{:S(2)}) collective-permute-start(bf16[64,4096]{1,0:T(8,128)(2,1)} %collective-permute-done.5.refs_3_), channel_id=1, source_target_pairs={{0,4},{2,6},{4,0},{6,2},{8,12},{10,14},{12,8},{14,10},{1,5},{3,7},... | collective-permute-start | bytes 1572872 | tf_op jit(solution)/shard_map/ppermute | solution.py:472
  89.6 82.4 %collective-permute-start.14 = (bf16[256,4096]{1,0:T(8,128)(2,1)}, bf16[256,4096]{1,0:T(8,128)(2,1)}, u32[]{:S(2)}, u32[]{:S(2)}) collective-permute-start(bf16[256,4096]{1,0:T(8,128)(2,1)} %get-tuple-element.31.refs_0_), channel_id=1, source_target_pairs={{0,1},{1,0},{2,3},{3,2},{4,5},{5,4},{6,7},{7,6},{8,9},{9,8},{10,11... | collective-permute-start | bytes 6291464 | tf_op jit(solution)/shard_map/ppermute | solution.py:472
  97.7 24.3 %collective-permute-start.11 = (s16[64,4224]{1,0:T(8,128)(2,1)}, s16[64,4224]{1,0:T(8,128)(2,1)S(1)}, u32[]{:S(2)}, u32[]{:S(2)}) collective-permute-start(s16[64,4224]{1,0:T(8,128)(2,1)} %get-tuple-element.28), channel_id=1, source_target_pairs={{0,4},{2,6},{4,0},{6,2},{8,12},{10,14},{12,8},{14,10},{1,5},{3,7},... | collective-permute-start | bytes 1622024 | tf_op jit(solution)/shard_map/ppermute | solution.py:472
  98.4 39.5 %collective-permute-start.12 = (s16[64,4224]{1,0:T(8,128)(2,1)}, s16[64,4224]{1,0:T(8,128)(2,1)}, u32[]{:S(2)}, u32[]{:S(2)}) collective-permute-start(s16[64,4224]{1,0:T(8,128)(2,1)} %get-tuple-element.29), channel_id=1, source_target_pairs={{0,8},{2,10},{4,12},{6,14},{8,0},{10,2},{12,4},{14,6},{1,9},{3,11}... | collective-permute-start | bytes 1622024 | tf_op jit(solution)/shard_map/ppermute | solution.py:472
  99.7 38.3 %collective-permute-start.13 = (s16[64,4224]{1,0:T(8,128)(2,1)}, s16[64,4224]{1,0:T(8,128)(2,1)}, u32[]{:S(2)}, u32[]{:S(2)}) collective-permute-start(s16[64,4224]{1,0:T(8,128)(2,1)} %get-tuple-element.30), channel_id=1, source_target_pairs={{0,12},{2,14},{4,8},{6,10},{8,4},{10,6},{12,0},{14,2},{1,13},{3,15... | collective-permute-start | bytes 1622024 | tf_op jit(solution)/shard_map/ppermute | solution.py:472
  122.0 50.0 %collective-permute-start.15 = (bf16[256,4096]{1,0:T(8,128)(2,1)}, bf16[256,4096]{1,0:T(8,128)(2,1)}, u32[]{:S(2)}, u32[]{:S(2)}) collective-permute-start(bf16[256,4096]{1,0:T(8,128)(2,1)} %get-tuple-element.32.refs_1_), channel_id=1, source_target_pairs={{0,1},{1,0},{2,3},{3,2},{4,5},{5,4},{6,7},{7,6},{8,9},{9,8},{10,11... | collective-permute-start | bytes 6291464 | tf_op jit(solution)/shard_map/ppermute | solution.py:472
  122.0 16.5 %copy-start = (s16[64,4224]{1,0:T(8,128)(2,1)}, s16[64,4224]{1,0:T(8,128)(2,1)S(1)}, u32[]{:S(2)}) copy-start(s16[64,4224]{1,0:T(8,128)(2,1)S(1)} %collective-permute-done.11.refs_1_.refs_2_) | copy-start | bytes 1622020
  122.0 44.1 %collective-permute-start.7 = (s16[256,3712]{1,0:T(8,128)(2,1)}, s16[256,3712]{1,0:T(8,128)(2,1)}, u32[]{:S(2)}, u32[]{:S(2)}) collective-permute-start(s16[256,3712]{1,0:T(8,128)(2,1)} %get-tuple-element.22), channel_id=1, source_target_pairs={{0,16},{16,0},{1,17},{17,1},{2,18},{18,2},{3,19},{19,3},{4,20},{20... | collective-permute-start | bytes 5701640 | tf_op jit(solution)/shard_map/ppermute | solution.py:472
  138.0 34.0 %collective-permute-start.16 = (bf16[256,3584]{1,0:T(8,128)(2,1)}, bf16[256,3584]{1,0:T(8,128)(2,1)}, u32[]{:S(2)}, u32[]{:S(2)}) collective-permute-start(bf16[256,3584]{1,0:T(8,128)(2,1)} %bitcast.25), channel_id=1, source_target_pairs={{0,1},{1,0},{2,3},{3,2},{4,5},{5,4},{6,7},{7,6},{8,9},{9,8},{10,11... | collective-permute-start | bytes 5505032 | tf_op jit(solution)/shard_map/ppermute | solution.py:472
  138.0 34.0 %collective-permute-start.17 = (bf16[256,3584]{1,0:T(8,128)(2,1)}, bf16[256,3584]{1,0:T(8,128)(2,1)}, u32[]{:S(2)}, u32[]{:S(2)}) collective-permute-start(bf16[256,3584]{1,0:T(8,128)(2,1)} %collective-permute-done.8.refs_0_.refs_1_.refs_2_.refs_3_.refs_5_), channel_id=1, source_target_pairs={{0,1},{1,0},{2,3},{3,2},{4,5},{5,4},{6,7},{7,6},{8,9},{9,8},{10,11... | collective-permute-start | bytes 5505032 | tf_op jit(solution)/shard_map/ppermute | solution.py:472

commit v3 on v2

--- a/solution.py
+++ b/solution.py
@@ -52,11 +52,11 @@
     return values.astype(jnp.int32).astype(jnp.int16)
 
 
-def strip_matmul(blocks, meta, weight, count_rows, count_cols, along_rows, coded, kept, gathered, instead=None):
+def strip_matmul(blocks, meta, weight, count_rows, count_cols, along_rows, coded, kept, gathered, swapped=None):
     builds = isinstance(weight, tuple)
     outer_tiles = count_rows if along_rows else count_cols
     width = next(w for w in (GROUP * 4, GROUP * 2, GROUP) if outer_tiles * TILE % w == 0)
-    if not along_rows or isinstance(weight, tuple):
+    if not along_rows:
         width = min(width, GROUP * 2)
     per = width // TILE
     steps = outer_tiles // per
@@ -74,8 +74,6 @@
     def kernel(meta, *refs):
         ins, refs = refs[: len(blocks)], refs[len(blocks) :]
         weight_ref, refs = refs[0], refs[1:]
-        if instead:
-            instead_ref, refs = refs[0], refs[1:]
         if coded:
             codes_ref, refs = refs[0], refs[1:]
         if kept:
@@ -85,19 +83,15 @@
         if builds:
             built_ref, refs = refs[0], refs[1:]
         held, refs = refs[0], refs[1:]
+        if coded:
+            waiting, refs = refs[0], refs[1:]
         step = pl.program_id(0)
 
         @pl.when(step == 0)
         def _():
             held[...] = jnp.zeros_like(held)
-
-        def mixed(here, there):
-            rows = coded // len(instead[2])
-            out = []
-            for (a, n), (b, m) in instead[2]:
-                one, two = (v[i * rows : (i + 1) * rows] for v, i in (((here, there)[a], n), ((here, there)[b], m)))
-                out.append(jnp.where(meta[instead[1]] == 1, one, two))
-            return jnp.concatenate(out, axis=0)
+            if coded:
+                waiting[1] = jnp.zeros((coded, width), jnp.float32)
 
         if builds:
             local, sems = refs
@@ -129,24 +123,29 @@
             y = lax.dot_general(x, strip, (((1,), (1,)), ((), ())), preferred_element_type=jnp.float32)
         else:
             y = jnp.dot(x, strip, preferred_element_type=jnp.float32)
+        first, last = y[:coded], y[first_kept:]
+        if swapped is not None:
+            turn = meta[swapped] == 1
+            first, last = jnp.where(turn, last, first), jnp.where(turn, first, last)
         if coded:
-            for g in range(width // GROUP):
-                codes, eighths = encode(y[:coded, g * GROUP : (g + 1) * GROUP])
-                here = pl.ds(pl.multiple_of(step * width + g * GROUP, GROUP), GROUP)
-                if instead:
-                    codes = mixed(codes, instead_ref[:, here])
-                codes_ref[:, here] = codes
-                held[...] = put_lane(held[...], eighths, step * (width // GROUP) + g)
+
+            def write_codes(values, step):
+                for g in range(width // GROUP):
+                    codes, eighths = encode(values[:, g * GROUP : (g + 1) * GROUP])
+                    here = pl.ds(pl.multiple_of(step * width + g * GROUP, GROUP), GROUP)
+                    codes_ref[:, here] = codes
+                    held[...] = put_lane(held[...], eighths, step * (width // GROUP) + g)
+
+            write_codes(waiting[1 - lax.rem(step, 2)], jnp.maximum(step - 1, 0))
+            waiting[lax.rem(step, 2)] = first
 
             @pl.when(step == steps - 1)
             def _():
-                last = pack(held[...])
-                if instead:
-                    last = mixed(last, instead_ref[:, outer:])
-                codes_ref[:, outer:] = last
+                write_codes(waiting[(steps - 1) % 2], steps - 1)
+                codes_ref[:, outer:] = pack(held[...])
 
         if kept:
-            kept_ref[...] = y[first_kept:]
+            kept_ref[...] = last
         if gathered:
 
             @pl.when(step == 0)
@@ -170,6 +169,8 @@
         outs.append(jax.ShapeDtypeStruct((tokens, inner), jnp.bfloat16))
         out_specs.append(pl.BlockSpec((tokens, inner), lambda s, m: (0, 0)))
     scratch = [pltpu.VMEM((max(coded, 8), LANES), jnp.float32)]
+    if coded:
+        scratch.append(pltpu.VMEM((2, coded, width), jnp.float32))
     strip_spec = pl.BlockSpec(strip_shape, (lambda s, m: (s, 0)) if along_rows else (lambda s, m: (0, s)))
     if builds:
         outs.append(jax.ShapeDtypeStruct((count_rows * TILE, count_cols * TILE), jnp.bfloat16))
@@ -183,8 +184,7 @@
             num_scalar_prefetch=1,
             grid=(steps,),
             in_specs=[in_spec(rows, entry) for _, rows, entry in blocks]
-            + [strip_spec]
-            + ([pl.BlockSpec((coded, outer + LANES), lambda s, m: (0, 0), pipeline_mode=pl.Buffered(1))] * bool(instead)),
+            + [strip_spec],
             out_specs=out_specs,
             scratch_shapes=scratch,
         ),
@@ -195,7 +195,7 @@
             transcendentals=0,
         ),
         name="dgrad" if along_rows else "forward",
-    )(meta, *[a for a, _, _ in blocks], tiles if builds else weight, *([instead[0]] if instead else []))
+    )(meta, *[a for a, _, _ in blocks], tiles if builds else weight)
 
 
 def tile_products(lefts, rights, meta, kept_tiles, count_rows, count_cols, factor, part, before):
@@ -230,42 +230,56 @@
             at = step * per * TILE
             return copies(lefts, left_refs, left_all, left_sems.at[step], first * TILE + at, at, per * TILE)
 
-        def right_copies():
-            return copies(rights, right_refs, right_all, right_sems, 0, 0, wide_cols)
+        pieces = [(b, min(4, count_cols - b)) for b in range(0, count_cols, 4)]
+
+        def right_copies(p):
+            at, width = pieces[p][0] * TILE, pieces[p][1] * TILE
+            return copies(rights, right_refs, right_all, right_sems.at[p], at, at, width)
+
+        def wait(group):
+            for c in group:
+                c.wait()
+
+        def work(opening):
+            now = 0 if opening else lax.rem(i, 2)
+            for p, (b, n) in enumerate(pieces):
+                if opening:
+                    wait(right_copies(p))
+                sums = jnp.dot(
+                    turned[now], right_all[:, b * TILE : (b + n) * TILE], preferred_element_type=jnp.float32
+                )
+                for a in range(per):
+                    for e in range(n):
+                        tile = meta[(first + i * per + a) * count_cols + b + e]
+                        found[tile] = sums[a * TILE : (a + 1) * TILE, e * TILE : (e + 1) * TILE] * factor
+            if opening:
+                for n in range(1, steps):
+                    wait(left_copies(n))
+            for a in range(per if steps > 1 else 0):
+                ahead = jnp.minimum(i + 1, steps - 1) * per + a
+                turned[1 - now, a * TILE : (a + 1) * TILE, :] = left_all[
+                    :, pl.ds(pl.multiple_of(ahead * TILE, TILE), TILE)
+                ].T
 
         @pl.when(i == 0)
         def _():
             for c in left_copies(0):
                 c.start()
-            for c in right_copies():
-                c.start()
+            for p in range(len(pieces)):
+                for c in right_copies(p):
+                    c.start()
             for n in range(1, steps):
                 for c in left_copies(n):
                     c.start()
-            for c in left_copies(0):
-                c.wait()
+            wait(left_copies(0))
             turned[0] = left_all[:, : per * TILE].T
-            for n in range(1, steps):
-                for c in left_copies(n):
-                    c.wait()
-            for c in right_copies():
-                c.wait()
-
-        now = lax.rem(i, 2)
-        for b in range(0, count_cols, 4):
-            n = min(4, count_cols - b)
-            sums = jnp.dot(
-                turned[now], right_all[:, b * TILE : (b + n) * TILE], preferred_element_type=jnp.float32
-            )
-            for a in range(per):
-                for e in range(n):
-                    tile = meta[(first + i * per + a) * count_cols + b + e]
-                    found[tile] = sums[a * TILE : (a + 1) * TILE, e * TILE : (e + 1) * TILE] * factor
-        for a in range(per if steps > 1 else 0):
-            ahead = jnp.minimum(i + 1, steps - 1) * per + a
-            turned[1 - now, a * TILE : (a + 1) * TILE, :] = left_all[
-                :, pl.ds(pl.multiple_of(ahead * TILE, TILE), TILE)
-            ].T
+            work(True)
+
+        if steps > 1:
+
+            @pl.when(i > 0)
+            def _():
+                work(False)
 
         def out_copies(low, high, begin):
             many = (high - low) // OUT_CHUNK
@@ -315,7 +329,7 @@
                 pltpu.VMEM((2, per * TILE, tokens), jnp.bfloat16),
                 pltpu.VMEM((kept_tiles + 1, TILE, TILE), jnp.float32),
                 pltpu.SemaphoreType.DMA((steps, sum(len(e) for _, _, e in lefts))),
-                pltpu.SemaphoreType.DMA((sum(len(e) for _, _, e in rights),)),
+                pltpu.SemaphoreType.DMA((-(-count_cols // 4), sum(len(e) for _, _, e in rights))),
                 pltpu.SemaphoreType.DMA((2,)),
             ],
         ),
@@ -332,7 +346,7 @@
 
 
 def add_received(locals_, received, sums, meta, rows, wide, sends, keep, keep_type):
-    span = 1024 if wide % 1024 == 0 else wide
+    span = wide if len(received) < 4 or wide % 2048 else 2048
     steps, groups = wide // span, span // GROUP
 
     def kernel(meta, *refs):
@@ -442,29 +456,17 @@
     return output, grad_input, grad_tiles[None, None]
 
 
-FIRST_SET, SECOND_SET = (0, 1, 2, 6), (3, 4, 5, 7)
-
-
-def block_pairs():
-    spot = {k: (1, n) for n, k in enumerate(FIRST_SET)} | {k: (0, n) for n, k in enumerate(SECOND_SET)}
-    return [(spot[n], spot[n + 4]) for n in range(4)]
-
-
 def pair_entries(row, col, size, groups):
     y, z0, z1 = col % 2, col // 2 % 2, col // 4
-    keep = [p[z1 != row] for p in (block_pairs()[n ^ (col % 4)] for n in range(4))]
     return {
         "dgrad": [1 - y, 3 - y, y, 2 + y],
-        "near": [int(z1 != row)],
+        "far": [int(z1 == row)],
         "z0": [z0, 1 - z0],
         "mine": [int(z1 == row)],
         "const": [0, 1],
-        "left": [g * size + (col ^ k) for g in range(groups) for k in FIRST_SET + SECOND_SET],
+        "left": [g * size + (col ^ k) for g in range(groups) for k in range(size)],
         "right": [2 * g + r for g in range(groups) for r in (row, 1 - row)],
         "codes": [n ^ (col % 4) for n in range(4)],
-        "second": [1 - k[0] for k in keep],
-        "in_first": [k[1] * k[0] for k in keep],
-        "in_second": [k[1] * (1 - k[0]) for k in keep],
     }
 
 
@@ -516,16 +518,22 @@
         blocks = [(grad, block, at["dgrad"] + e) for e in range(4)]
         return strip_matmul(blocks, meta, weight, count_rows, count_cols, True, 2 * block, 2 * block, False)
 
-    def forward(blocks, weight, instead):
-        blocks = [(b, block, None) for b in blocks]
-        return strip_matmul(blocks, meta, weight, count_rows, count_cols, False, half, half, True, instead)
-
     codes_mine, kept_mine, weight = dgrad(grad_mine, (tiles,))
     codes_mine = swap_col(codes_mine, 1)
-    first_codes, first_kept, first_act = forward([own, b1, b2, b6], weight, None)
     codes_other, kept_other = dgrad(grad_other, weight)
     codes_other = swap_col(codes_other, 1)
-    out_codes, second_kept, second_act = forward([b3, b4, b5, b7], weight, (first_codes, at["near"], block_pairs()))
+    out_codes, out_kept, act = strip_matmul(
+        [(b, block, None) for b in (own, b1, b2, b3, b4, b5, b6, b7)],
+        meta,
+        weight,
+        count_rows,
+        count_cols,
+        False,
+        half,
+        half,
+        True,
+        at["far"],
+    )
     out_codes = swap_row(out_codes)
 
     z0, const, mine = at["z0"], at["const"], at["mine"]
@@ -546,12 +554,9 @@
     )
     codes = [swap_col(v, 2 * n + 2) for n, v in enumerate(codes)]
 
-    partner = [swap_depth(v) for v in (first_act, second_act, grad_mine, grad_other)]
-    lefts = [
-        (v, block, [at["left"] + 4 * n + k for k in range(4)])
-        for n, v in enumerate((first_act, second_act, *partner[:2]))
-    ]
-    rights = [(v, half, [at["right"] + n]) for n, v in enumerate((grad_mine, grad_other, *partner[2:]))]
+    partner = [swap_depth(v) for v in (act, grad_mine, grad_other)]
+    lefts = [(v, block, [at["left"] + size * n + k for k in range(size)]) for n, v in enumerate((act, partner[0]))]
+    rights = [(v, half, [at["right"] + n]) for n, v in enumerate((grad_mine, grad_other, *partner[1:]))]
 
     def wgrad(part, before):
         return tile_products(
@@ -578,21 +583,19 @@
         lambda s, m: s[0],
         jnp.bfloat16,
     )
-    output = join_output(first_kept, second_kept, out_codes, meta, at, block)
+    output = join_output(out_kept, out_codes, meta, at["codes"], block)
     return output[None], grad_input[None], grad_tiles[None, None]
 
 
-def join_output(first, second, codes, meta, at, rows):
-    wide = first.shape[1]
-    blocks = first.shape[0] // rows
-
-    def kernel(meta, first_ref, second_ref, codes_ref, out_ref):
-        use_second = meta[at["second"] + pl.program_id(0)] == 1
+def join_output(local, codes, meta, first, rows):
+    wide = local.shape[1]
+    blocks = local.shape[0] // rows
+
+    def kernel(meta, local_ref, codes_ref, out_ref):
         for g in range(wide // GROUP):
             here = slice(g * GROUP, (g + 1) * GROUP)
-            local = jnp.where(use_second, second_ref[:, here], first_ref[:, here])
             eighths = pick_lane(codes_ref[:, wide:], g)
-            out_ref[:, here] = (local + decode(codes_ref[:, here], eighths)).astype(jnp.bfloat16)
+            out_ref[:, here] = (local_ref[:, here] + decode(codes_ref[:, here], eighths)).astype(jnp.bfloat16)
 
     return pl.pallas_call(
         kernel,
@@ -601,16 +604,15 @@
             num_scalar_prefetch=1,
             grid=(blocks,),
             in_specs=[
-                pl.BlockSpec((rows, wide), lambda n, m: (m[at["in_first"] + n], 0)),
-                pl.BlockSpec((rows, wide), lambda n, m: (m[at["in_second"] + n], 0)),
-                pl.BlockSpec((rows, wide + LANES), lambda n, m: (m[at["codes"] + n], 0)),
+                pl.BlockSpec((rows, wide), lambda n, m: (m[first + n], 0)),
+                pl.BlockSpec((rows, wide + LANES), lambda n, m: (m[first + n], 0)),
             ],
             out_specs=pl.BlockSpec((rows, wide), lambda n, m: (n, 0)),
         ),
         compiler_params=params(),
-        cost_estimate=pl.CostEstimate(flops=8 * first.size, bytes_accessed=first.size * 8, transcendentals=0),
+        cost_estimate=pl.CostEstimate(flops=8 * local.size, bytes_accessed=local.size * 8, transcendentals=0),
         name="join_output",
-    )(meta, first, second, codes)
+    )(meta, local, codes)
 
 
 def solution(mesh):

time: 216 us -> 260 us (1.20)
  the two profiles are of different devices: /device:TPU:0 before, /device:TPU:8 now
where the time goes in v3:
time: 260 us; the launch traced here: 259 us
  waiting for transfers between devices  122 us (47%)
  Pallas kernels  117 us (45%)
  starting transfers between devices  16.3 us (6%)
    ppermute x17, waiting for transfers between devices, swap(): return lax.ppermute(value, axis, [(i, i ^ bit) for i in range(size)])  122 us
    pallas_call x3, Pallas kernels, strip_matmul(): pl.pallas_call(kernel, out_shape=outs, grid_spec=pltpu.PrefetchScalarGrid...  59.3 us
    pallas_call x1, Pallas kernels, tile_products(): pl.pallas_call(kernel, out_shape=jax.ShapeDtypeStruct((kept_tiles, TILE,...  41.6 us
    ppermute x17, starting transfers between devices, swap(): return lax.ppermute(value, axis, [(i, i ^ bit) for i in range(size)])  16.3 us
    pallas_call x2, Pallas kernels, add_received(): pl.pallas_call(kernel, out_shape=outs, grid_spec=pltpu.PrefetchScalarGrid...  10.5 us
    pallas_call x1, Pallas kernels, join_output(): pl.pallas_call(kernel, out_shape=jax.ShapeDtypeStruct((blocks * rows, wid...  5.4 us
  transfers between devices with their start and end apart: 17, of which 8 were waited for; matrix products, arithmetic and copies ran while one was open for 1% of the time, Pallas kernels for 29%

profile of v3, /device:TPU:8, one launch (start us, length us, event | category | flops | bytes accessed | tf_op | source)
XLA Modules:
  0.0 258.9 jit_solution(3743731410271198936)
XLA Ops:
  0.6 1.6 collective-permute-start.3
  2.3 1.5 collective-permute-start
  3.8 2.5 collective-permute-start.1
  6.3 1.5 collective-permute-start.8
  9.3 16.5 %collective-permute-done.3.refs_6_ = bf16[64,4096]{1,0:T(8,128)(2,1)S(1)} collective-permute-done((bf16[64,4096]{1,0:T(8,128)(2,1)}, bf16[64,4096]{1,0:T(8,128)(2,1)S(1)}, u32[]{:S(2)}, u32[]{:S(2)}) %collective-permute-start.3) | collective-permute-done | bytes 524320 | tf_op jit(solution)/shard_map/ppermute | solution.py:474
  25.8 1.5 collective-permute-start.5
  28.9 2.0 collective-permute-start.2
  31.0 8.0 %collective-permute-done.5.refs_7_ = bf16[64,4096]{1,0:T(8,128)(2,1)} collective-permute-done((bf16[64,4096]{1,0:T(8,128)(2,1)S(1)}, bf16[64,4096]{1,0:T(8,128)(2,1)}, u32[]{:S(2)}, u32[]{:S(2)}) %collective-permute-start.5) | collective-permute-done | bytes 524320 | tf_op jit(solution)/shard_map/ppermute | solution.py:474
  39.0 18.7 %dgrad.2 = (s16[128,4224]{1,0:T(8,128)(2,1)}, f32[128,4096]{1,0:T(8,128)}, bf16[4096,3584]{1,0:T(8,128)(2,1)}) custom-call(s32[963]{0:T(1024)} %pad_add_fusion.meta, bf16[256,3584]{1,0:T(8,128)(2,1)} %bitcast.17, bf16[256,3584]{1,0:T(8,128)(2,1)} %bitcast.18, bf16[256,3584]{1,0:T(8,128)(2,1)} %bitcast.19, bf16[256,3584]{1,0:T(8,128)(2,1)} %bitcast.20, ...), custom_call_target="tpu_custom_call" | custom-call | flops 7516192768 | bytes 35389440 | tf_op jit(solution)/shard_map/dgrad/pallas_call | solution.py:180
  57.7 6.6 %collective-permute-done.6.refs_5_ = bf16[64,4096]{1,0:T(8,128)(2,1)} collective-permute-done((bf16[64,4096]{1,0:T(8,128)(2,1)}, bf16[64,4096]{1,0:T(8,128)(2,1)}, u32[]{:S(2)}, u32[]{:S(2)}) %collective-permute-start.6) | collective-permute-done | bytes 524320 | tf_op jit(solution)/shard_map/ppermute | solution.py:474
  64.3 24.7 %forward.1 = (s16[256,3712]{1,0:T(8,128)(2,1)}, f32[256,3584]{1,0:T(8,128)}, bf16[512,4096]{1,0:T(8,128)(2,1)}) custom-call(s32[963]{0:T(1024)} %pad_add_fusion.meta, bf16[64,4096]{1,0:T(8,128)(2,1)} %bitcast.26, bf16[64,4096]{1,0:T(8,128)(2,1)} %collective-permute-done.refs_1_, bf16[64,4096]{1,0:T(8,128)(2,1)} %collective-permute-done.1.refs_2_, ...), custom_call_target="tpu_custom_call" | custom-call | flops 15032385536 | bytes 40894464 | tf_op jit(solution)/shard_map/forward/pallas_call | solution.py:180
  89.6 15.9 %dgrad.3 = (s16[128,4224]{1,0:T(8,128)(2,1)}, f32[128,4096]{1,0:T(8,128)}) custom-call(s32[963]{0:T(1024)} %pad_add_fusion.meta, bf16[256,3584]{1,0:T(8,128)(2,1)} %collective-permute-done.8.refs_0_.refs_1_.refs_2_.refs_3_, bf16[256,3584]{1,0:T(8,128)(2,1)} %collective-permute-done.8.refs_0_.refs_1_.refs_2_.refs_3_, ...), custom_call_target="tpu_custom_call" | custom-call | flops 7516192768 | bytes 35389440 | tf_op jit(solution)/shard_map/dgrad/pallas_call | solution.py:180
  105.6 1.5 collective-permute-start.10
  107.1 1.5 collective-permute-start.7
  108.6 7.6 %collective-permute-done.9.refs_4_.refs_5_.refs_6_.refs_7_ = s16[128,4224]{1,0:T(8,128)(2,1)} collective-permute-done((s16[128,4224]{1,0:T(8,128)(2,1)}, s16[128,4224]{1,0:T(8,128)(2,1)}, u32[]{:S(2)}, u32[]{:S(2)}) %collective-permute-start.9) | collective-permute-done | bytes 1081376 | tf_op jit(solution)/shard_map/ppermute | solution.py:474
  116.2 22.6 %collective-permute-done.10.refs_8_.refs_9_.refs_10_.refs_11_ = s16[128,4224]{1,0:T(8,128)(2,1)} collective-permute-done((s16[128,4224]{1,0:T(8,128)(2,1)}, s16[128,4224]{1,0:T(8,128)(2,1)}, u32[]{:S(2)}, u32[]{:S(2)}) %collective-permute-start.10) | collective-permute-done | bytes 1081376 | tf_op jit(solution)/shard_map/ppermute | solution.py:474
  138.8 6.6 %add_received.2 = (s16[64,4224]{1,0:T(8,128)(2,1)}, s16[64,4224]{1,0:T(8,128)(2,1)}, s16[64,4224]{1,0:T(8,128)(2,1)}, f32[64,4096]{1,0:T(8,128)}) custom-call(s32[963]{0:T(1024)} %pad_add_fusion.meta, f32[128,4096]{1,0:T(8,128)} %get-tuple-element.18.refs_0_.refs_1_, f32[128,4096]{1,0:T(8,128)} %get-tuple-element.18.refs_0_.refs_1_, ...), custom_call_target="tpu_custom_call" | custom-call | flops 2097152 | bytes 9437184 | tf_op jit(solution)/shard_map/add_received/pallas_call | solution.py:395
  145.8 13.7 %collective-permute-done.11.refs_1_.refs_2_ = s16[64,4224]{1,0:T(8,128)(2,1)S(1)} collective-permute-done((s16[64,4224]{1,0:T(8,128)(2,1)}, s16[64,4224]{1,0:T(8,128)(2,1)S(1)}, u32[]{:S(2)}, u32[]{:S(2)}) %collective-permute-start.11) | collective-permute-done | bytes 540704 | tf_op jit(solution)/shard_map/ppermute | solution.py:474
  159.5 1.1 collective-permute-start.12
  160.6 22.4 %collective-permute-done.12.refs_3_.refs_4_ = s16[64,4224]{1,0:T(8,128)(2,1)} collective-permute-done((s16[64,4224]{1,0:T(8,128)(2,1)}, s16[64,4224]{1,0:T(8,128)(2,1)}, u32[]{:S(2)}, u32[]{:S(2)}) %collective-permute-start.12) | collective-permute-done | bytes 540704 | tf_op jit(solution)/shard_map/ppermute | solution.py:474
  183.6 24.3 %collective-permute-done.13.refs_5_.refs_6_ = s16[64,4224]{1,0:T(8,128)(2,1)} collective-permute-done((s16[64,4224]{1,0:T(8,128)(2,1)}, s16[64,4224]{1,0:T(8,128)(2,1)}, u32[]{:S(2)}, u32[]{:S(2)}) %collective-permute-start.13) | collective-permute-done | bytes 540704 | tf_op jit(solution)/shard_map/ppermute | solution.py:474
  207.9 3.9 %add_received.3 = bf16[64,4096]{1,0:T(8,128)(2,1)} custom-call(s32[963]{0:T(1024)} %pad_add_fusion.meta, f32[64,4096]{1,0:T(8,128)} %get-tuple-element.22.refs_0_, s16[64,4224]{1,0:T(8,128)(2,1)} %copy-done, s16[64,4224]{1,0:T(8,128)(2,1)} %copy-done, s16[64,4224]{1,0:T(8,128)(2,1)} %collective-permute-done.12.refs_3_.refs_4_, ...), custom_call_target="tpu_custom_call" | custom-call | flops 2097152 | bytes 5505024 | tf_op jit(solution)/shard_map/add_received/pallas_call | solution.py:395
  211.7 5.4 %join_output.1 = bf16[256,3584]{1,0:T(8,128)(2,1)} custom-call(s32[963]{0:T(1024)} %pad_add_fusion.meta, f32[256,3584]{1,0:T(8,128)} %get-tuple-element.16.local_ref, s16[256,3712]{1,0:T(8,128)(2,1)} %collective-permute-done.7.codes_ref), custom_call_target="tpu_custom_call" | custom-call | flops 7340032 | bytes 7340032 | tf_op jit(solution)/shard_map/join_output/pallas_call | solution.py:600
  217.2 41.6 %wgrad.1 = f32[448,128,128]{2,1,0:T(8,128)} custom-call(s32[963]{0:T(1024)} %pad_add_fusion.meta, bf16[512,4096]{1,0:T(8,128)(2,1)} %get-tuple-element.26.refs_0_, bf16[512,4096]{1,0:T(8,128)(2,1)} %collective-permute-done.14.refs_1_, bf16[256,3584]{1,0:T(8,128)(2,1)} %bitcast.22, bf16[256,3584]{1,0:T(8,128)(2,1)} %collective-permute-done.8.refs_0_.refs_1_.refs_2_.refs_3_, ...), custom_call_target="tpu_custom_call" | custom-call | flops 30064771072 | bytes 45088768 | tf_op jit(solution)/shard_map/wgrad/pallas_call | solution.py:318
  (27 shorter events, 4.6 us)
Async XLA Ops:
  0.6 25.2 %collective-permute-start.3 = (bf16[64,4096]{1,0:T(8,128)(2,1)}, bf16[64,4096]{1,0:T(8,128)(2,1)S(1)}, u32[]{:S(2)}, u32[]{:S(2)}) collective-permute-start(bf16[64,4096]{1,0:T(8,128)(2,1)} %bitcast.23), channel_id=1, source_target_pairs={{0,12},{2,14},{4,8},{6,10},{8,4},{10,6},{12,0},{14,2},{1,13},{3,15... | collective-permute-start | bytes 1572872 | tf_op jit(solution)/shard_map/ppermute | solution.py:474
  2.3 26.7 %collective-permute-start = (bf16[64,4096]{1,0:T(8,128)(2,1)}, bf16[64,4096]{1,0:T(8,128)(2,1)}, u32[]{:S(2)}, u32[]{:S(2)}) collective-permute-start(bf16[64,4096]{1,0:T(8,128)(2,1)} %bitcast.24), channel_id=1, source_target_pairs={{0,2},{2,0},{4,6},{6,4},{8,10},{10,8},{12,14},{14,12},{1,3},{3,1},... | collective-permute-start | bytes 1572872 | tf_op jit(solution)/shard_map/ppermute | solution.py:474
  3.8 53.9 %collective-permute-start.1 = (bf16[64,4096]{1,0:T(8,128)(2,1)}, bf16[64,4096]{1,0:T(8,128)(2,1)}, u32[]{:S(2)}, u32[]{:S(2)}) collective-permute-start(bf16[64,4096]{1,0:T(8,128)(2,1)} %bitcast.25), channel_id=1, source_target_pairs={{0,4},{2,6},{4,0},{6,2},{8,12},{10,14},{12,8},{14,10},{1,5},{3,7},... | collective-permute-start | bytes 1572872 | tf_op jit(solution)/shard_map/ppermute | solution.py:474
  6.3 83.4 %collective-permute-start.8 = (bf16[256,3584]{1,0:T(8,128)(2,1)}, bf16[256,3584]{1,0:T(8,128)(2,1)}, u32[]{:S(2)}, u32[]{:S(2)}) collective-permute-start(bf16[256,3584]{1,0:T(8,128)(2,1)} %bitcast.16), channel_id=1, source_target_pairs={{0,16},{16,0},{1,17},{17,1},{2,18},{18,2},{3,19},{19,3},{4,20},{20... | collective-permute-start | bytes 5505032 | tf_op jit(solution)/shard_map/ppermute | solution.py:474
  25.8 31.9 %copy-start.1 = (bf16[64,4096]{1,0:T(8,128)(2,1)}, bf16[64,4096]{1,0:T(8,128)(2,1)S(1)}, u32[]{:S(2)}) copy-start(bf16[64,4096]{1,0:T(8,128)(2,1)S(1)} %collective-permute-done.3.refs_6_) | copy-start | bytes 1572868
  25.8 13.2 %collective-permute-start.5 = (bf16[64,4096]{1,0:T(8,128)(2,1)S(1)}, bf16[64,4096]{1,0:T(8,128)(2,1)}, u32[]{:S(2)}, u32[]{:S(2)}) collective-permute-start(bf16[64,4096]{1,0:T(8,128)(2,1)S(1)} %collective-permute-done.3.refs_6_), channel_id=1, source_target_pairs={{0,2},{2,0},{4,6},{6,4},{8,10},{10,8},{12,14},{14,12},{1,3},{3,1},... | collective-permute-start | bytes 1572872 | tf_op jit(solution)/shard_map/ppermute | solution.py:474
  28.9 28.8 %collective-permute-start.4 = (bf16[64,4096]{1,0:T(8,128)(2,1)S(1)}, bf16[64,4096]{1,0:T(8,128)(2,1)}, u32[]{:S(2)}, u32[]{:S(2)}) collective-permute-start(bf16[64,4096]{1,0:T(8,128)(2,1)S(1)} %collective-permute-done.3.refs_6_), channel_id=1, source_target_pairs={{0,4},{2,6},{4,0},{6,2},{8,12},{10,14},{12,8},{14,10},{1,5},{3,7},... | collective-permute-start | bytes 1572872 | tf_op jit(solution)/shard_map/ppermute | solution.py:474
  28.9 28.8 %collective-permute-start.2 = (bf16[64,4096]{1,0:T(8,128)(2,1)}, bf16[64,4096]{1,0:T(8,128)(2,1)}, u32[]{:S(2)}, u32[]{:S(2)}) collective-permute-start(bf16[64,4096]{1,0:T(8,128)(2,1)} %collective-permute-done.refs_1_), channel_id=1, source_target_pairs={{0,4},{2,6},{4,0},{6,2},{8,12},{10,14},{12,8},{14,10},{1,5},{3,7},... | collective-permute-start | bytes 1572872 | tf_op jit(solution)/shard_map/ppermute | solution.py:474
  39.0 25.3 %collective-permute-start.6 = (bf16[64,4096]{1,0:T(8,128)(2,1)}, bf16[64,4096]{1,0:T(8,128)(2,1)}, u32[]{:S(2)}, u32[]{:S(2)}) collective-permute-start(bf16[64,4096]{1,0:T(8,128)(2,1)} %collective-permute-done.5.refs_7_), channel_id=1, source_target_pairs={{0,4},{2,6},{4,0},{6,2},{8,12},{10,14},{12,8},{14,10},{1,5},{3,7},... | collective-permute-start | bytes 1572872 | tf_op jit(solution)/shard_map/ppermute | solution.py:474
  89.0 128.1 %collective-permute-start.14 = (bf16[512,4096]{1,0:T(8,128)(2,1)}, bf16[512,4096]{1,0:T(8,128)(2,1)}, u32[]{:S(2)}, u32[]{:S(2)}) collective-permute-start(bf16[512,4096]{1,0:T(8,128)(2,1)} %get-tuple-element.26.refs_0_), channel_id=1, source_target_pairs={{0,1},{1,0},{2,3},{3,2},{4,5},{5,4},{6,7},{7,6},{8,9},{9,8},{10,11... | collective-permute-start | bytes 12582920 | tf_op jit(solution)/shard_map/ppermute | solution.py:474
  89.1 27.1 %collective-permute-start.9 = (s16[128,4224]{1,0:T(8,128)(2,1)}, s16[128,4224]{1,0:T(8,128)(2,1)}, u32[]{:S(2)}, u32[]{:S(2)}) collective-permute-start(s16[128,4224]{1,0:T(8,128)(2,1)} %get-tuple-element.20), channel_id=1, source_target_pairs={{0,2},{2,0},{4,6},{6,4},{8,10},{10,8},{12,14},{14,12},{1,3},{3,1},... | collective-permute-start | bytes 3244040 | tf_op jit(solution)/shard_map/ppermute | solution.py:474
  105.6 33.2 %collective-permute-start.10 = (s16[128,4224]{1,0:T(8,128)(2,1)}, s16[128,4224]{1,0:T(8,128)(2,1)}, u32[]{:S(2)}, u32[]{:S(2)}) collective-permute-start(s16[128,4224]{1,0:T(8,128)(2,1)} %get-tuple-element.21), channel_id=1, source_target_pairs={{0,2},{2,0},{4,6},{6,4},{8,10},{10,8},{12,14},{14,12},{1,3},{3,1},... | collective-permute-start | bytes 3244040 | tf_op jit(solution)/shard_map/ppermute | solution.py:474
  107.1 104.6 %collective-permute-start.7 = (s16[256,3712]{1,0:T(8,128)(2,1)}, s16[256,3712]{1,0:T(8,128)(2,1)}, u32[]{:S(2)}, u32[]{:S(2)}) collective-permute-start(s16[256,3712]{1,0:T(8,128)(2,1)} %get-tuple-element.17), channel_id=1, source_target_pairs={{0,16},{16,0},{1,17},{17,1},{2,18},{18,2},{3,19},{19,3},{4,20},{20... | collective-permute-start | bytes 5701640 | tf_op jit(solution)/shard_map/ppermute | solution.py:474
  108.6 108.5 %collective-permute-start.15 = (bf16[256,3584]{1,0:T(8,128)(2,1)}, bf16[256,3584]{1,0:T(8,128)(2,1)}, u32[]{:S(2)}, u32[]{:S(2)}) collective-permute-start(bf16[256,3584]{1,0:T(8,128)(2,1)} %bitcast.21), channel_id=1, source_target_pairs={{0,1},{1,0},{2,3},{3,2},{4,5},{5,4},{6,7},{7,6},{8,9},{9,8},{10,11... | collective-permute-start | bytes 5505032 | tf_op jit(solution)/shard_map/ppermute | solution.py:474
  116.2 101.0 %collective-permute-start.16 = (bf16[256,3584]{1,0:T(8,128)(2,1)}, bf16[256,3584]{1,0:T(8,128)(2,1)}, u32[]{:S(2)}, u32[]{:S(2)}) collective-permute-start(bf16[256,3584]{1,0:T(8,128)(2,1)} %collective-permute-done.8.refs_0_.refs_1_.refs_2_.refs_3_), channel_id=1, source_target_pairs={{0,1},{1,0},{2,3},{3,2},{4,5},{5,4},{6,7},{7,6},{8,9},{9,8},{10,11... | collective-permute-start | bytes 5505032 | tf_op jit(solution)/shard_map/ppermute | solution.py:474
  145.5 14.0 %collective-permute-start.11 = (s16[64,4224]{1,0:T(8,128)(2,1)}, s16[64,4224]{1,0:T(8,128)(2,1)S(1)}, u32[]{:S(2)}, u32[]{:S(2)}) collective-permute-start(s16[64,4224]{1,0:T(8,128)(2,1)} %get-tuple-element.23), channel_id=1, source_target_pairs={{0,4},{2,6},{4,0},{6,2},{8,12},{10,14},{12,8},{14,10},{1,5},{3,7},... | collective-permute-start | bytes 1622024 | tf_op jit(solution)/shard_map/ppermute | solution.py:474
  159.5 48.4 %copy-start = (s16[64,4224]{1,0:T(8,128)(2,1)}, s16[64,4224]{1,0:T(8,128)(2,1)S(1)}, u32[]{:S(2)}) copy-start(s16[64,4224]{1,0:T(8,128)(2,1)S(1)} %collective-permute-done.11.refs_1_.refs_2_) | copy-start | bytes 1622020
  159.5 23.5 %collective-permute-start.12 = (s16[64,4224]{1,0:T(8,128)(2,1)}, s16[64,4224]{1,0:T(8,128)(2,1)}, u32[]{:S(2)}, u32[]{:S(2)}) collective-permute-start(s16[64,4224]{1,0:T(8,128)(2,1)} %get-tuple-element.24), channel_id=1, source_target_pairs={{0,8},{2,10},{4,12},{6,14},{8,0},{10,2},{12,4},{14,6},{1,9},{3,11}... | collective-permute-start | bytes 1622024 | tf_op jit(solution)/shard_map/ppermute | solution.py:474
  183.0 24.8 %collective-permute-start.13 = (s16[64,4224]{1,0:T(8,128)(2,1)}, s16[64,4224]{1,0:T(8,128)(2,1)}, u32[]{:S(2)}, u32[]{:S(2)}) collective-permute-start(s16[64,4224]{1,0:T(8,128)(2,1)} %get-tuple-element.25), channel_id=1, source_target_pairs={{0,12},{2,14},{4,8},{6,10},{8,4},{10,6},{12,0},{14,2},{1,13},{3,15... | collective-permute-start | bytes 1622024 | tf_op jit(solution)/shard_map/ppermute | solution.py:474

commit v4 on v3

--- a/solution.py
+++ b/solution.py
@@ -17,7 +17,8 @@
 OUT_CHUNK = 16
 LEVELS = 32600.0
 SMALL = 1e-30
-VMEM_LIMIT = 63 * 1024 * 1024
+VMEM_LIMIT = 67000000
+STRIP_LIMIT = 67000000
 
 
 def params(limit=VMEM_LIMIT):
@@ -31,17 +32,23 @@
     return pack(codes), eighths
 
 
-def decode(codes, eighths):
-    return codes.astype(jnp.int32).astype(jnp.float32) * jnp.exp2(eighths * 0.125)
+def decode(codes, scale):
+    return codes.astype(jnp.int32).astype(jnp.float32) * scale
+
+
+def scales_of(last):
+    return jnp.exp2(last.astype(jnp.int32).astype(jnp.float32) * 0.125)
 
 
 def lane_of(shape):
     return lax.broadcasted_iota(jnp.int32, shape, len(shape) - 1)
 
 
-def pick_lane(values, lane):
-    values = values.astype(jnp.int32).astype(jnp.float32)
-    return jnp.sum(jnp.where(lane_of(values.shape) == lane, values, 0.0), axis=1, keepdims=True)
+def column_of(scales, step, steps, groups, g):
+    column = scales[:, g : g + 1]
+    for n in range(1, steps):
+        column = jnp.where(step == n, scales[:, n * groups + g : n * groups + g + 1], column)
+    return column
 
 
 def put_lane(values, column, lane):
@@ -85,7 +92,26 @@
         held, refs = refs[0], refs[1:]
         if coded:
             waiting, refs = refs[0], refs[1:]
+        if gathered:
+            gathered_sems, refs = refs[0], refs[1:]
         step = pl.program_id(0)
+
+        def gathered_copies():
+            for n, ref in enumerate(ins):
+                rows = blocks[n][1]
+                yield pltpu.make_async_copy(ref, gathered_ref.at[pl.ds(n * rows, rows), :], gathered_sems.at[n])
+
+        if gathered:
+
+            @pl.when(step == 0)
+            def _():
+                for c in gathered_copies():
+                    c.start()
+
+            @pl.when(step == steps - 1)
+            def _():
+                for c in gathered_copies():
+                    c.wait()
 
         @pl.when(step == 0)
         def _():
@@ -146,11 +172,6 @@
 
         if kept:
             kept_ref[...] = last
-        if gathered:
-
-            @pl.when(step == 0)
-            def _():
-                gathered_ref[...] = x
 
     def in_spec(rows, entry):
         def place(step, meta):
@@ -167,10 +188,12 @@
         out_specs.append(pl.BlockSpec((kept, width), lambda s, m: (0, s)))
     if gathered:
         outs.append(jax.ShapeDtypeStruct((tokens, inner), jnp.bfloat16))
-        out_specs.append(pl.BlockSpec((tokens, inner), lambda s, m: (0, 0)))
+        out_specs.append(pl.BlockSpec(memory_space=pl.ANY))
     scratch = [pltpu.VMEM((max(coded, 8), LANES), jnp.float32)]
     if coded:
         scratch.append(pltpu.VMEM((2, coded, width), jnp.float32))
+    if gathered:
+        scratch.append(pltpu.SemaphoreType.DMA((len(blocks),)))
     strip_spec = pl.BlockSpec(strip_shape, (lambda s, m: (s, 0)) if along_rows else (lambda s, m: (0, s)))
     if builds:
         outs.append(jax.ShapeDtypeStruct((count_rows * TILE, count_cols * TILE), jnp.bfloat16))
@@ -188,7 +211,7 @@
             out_specs=out_specs,
             scratch_shapes=scratch,
         ),
-        compiler_params=params(),
+        compiler_params=params(STRIP_LIMIT),
         cost_estimate=pl.CostEstimate(
             flops=2 * tokens * inner * outer,
             bytes_accessed=inner * outer * 2 + tokens * (inner * 2 + outer * 4),
@@ -359,6 +382,8 @@
         def _():
             held[...] = jnp.zeros_like(held)
 
+        scales = [scales_of(code_refs[2 * n + 1][...]) for n in range(len(received))]
+        marks = [held[n] for n in range(len(sends))]
         for g in range(groups):
             here = slice(g * GROUP, (g + 1) * GROUP)
             there = pl.ds(pl.multiple_of(step * span + g * GROUP, GROUP), GROUP)
@@ -366,14 +391,16 @@
             for local, others in sums:
                 total = local_refs[local][:, here]
                 for n in others:
-                    eighths = pick_lane(code_refs[2 * n + 1][...], step * groups + g)
-                    total = total + decode(code_refs[2 * n][:, here], eighths)
+                    scale = column_of(scales[n], step, steps, groups, g)
+                    total = total + decode(code_refs[2 * n][:, here], scale)
                 totals.append(total)
             keep_ref[:, here] = keep(totals, meta).astype(keep_type)
             for n, send in enumerate(sends):
                 codes, eighths = encode(send(totals, meta))
                 send_refs[n][:, there] = codes
-                held[n] = put_lane(held[n], eighths, step * groups + g)
+                marks[n] = put_lane(marks[n], eighths, step * groups + g)
+        for n, mark in enumerate(marks):
+            held[n] = mark
 
         @pl.when(step == steps - 1)
         def _():
@@ -592,10 +619,11 @@
     blocks = local.shape[0] // rows
 
     def kernel(meta, local_ref, codes_ref, out_ref):
+        scales = scales_of(codes_ref[:, wide:])
         for g in range(wide // GROUP):
             here = slice(g * GROUP, (g + 1) * GROUP)
-            eighths = pick_lane(codes_ref[:, wide:], g)
-            out_ref[:, here] = (local_ref[:, here] + decode(codes_ref[:, here], eighths)).astype(jnp.bfloat16)
+            total = local_ref[:, here] + decode(codes_ref[:, here], scales[:, g : g + 1])
+            out_ref[:, here] = total.astype(jnp.bfloat16)
 
     return pl.pallas_call(
         kernel,

time: 260 us -> 259 us (level)
  no operation moved by 1% of the time
where the time goes in v4:
time: 259 us; the launch traced here: 258 us
  waiting for transfers between devices  122 us (47%)
  Pallas kernels  116 us (45%)
  starting transfers between devices  16.3 us (6%)
    ppermute x17, waiting for transfers between devices, swap(): return lax.ppermute(value, axis, [(i, i ^ bit) for i in range(size)])  122 us
    pallas_call x3, Pallas kernels, strip_matmul(): pl.pallas_call(kernel, out_shape=outs, grid_spec=pltpu.PrefetchScalarGrid...  58 us
    pallas_call x1, Pallas kernels, tile_products(): pl.pallas_call(kernel, out_shape=jax.ShapeDtypeStruct((kept_tiles, TILE,...  41.6 us
    ppermute x17, starting transfers between devices, swap(): return lax.ppermute(value, axis, [(i, i ^ bit) for i in range(size)])  16.3 us
    pallas_call x2, Pallas kernels, add_received(): pl.pallas_call(kernel, out_shape=outs, grid_spec=pltpu.PrefetchScalarGrid...  11 us
    pallas_call x1, Pallas kernels, join_output(): pl.pallas_call(kernel, out_shape=jax.ShapeDtypeStruct((blocks * rows, wid...  5.4 us
  transfers between devices with their start and end apart: 17, of which 8 were waited for; matrix products, arithmetic and copies ran while one was open for 1% of the time, Pallas kernels for 29%

profile of v4, /device:TPU:8, one launch (start us, length us, event | category | flops | bytes accessed | tf_op | source)
XLA Modules:
  0.0 258.4 jit_solution(10526646989031216423)
XLA Ops:
  0.6 1.6 collective-permute-start.3
  2.3 1.5 collective-permute-start
  3.8 2.5 collective-permute-start.1
  6.3 1.5 collective-permute-start.8
  9.3 16.6 %collective-permute-done.3.refs_6_ = bf16[64,4096]{1,0:T(8,128)(2,1)} collective-permute-done((bf16[64,4096]{1,0:T(8,128)(2,1)}, bf16[64,4096]{1,0:T(8,128)(2,1)}, u32[]{:S(2)}, u32[]{:S(2)}) %collective-permute-start.3) | collective-permute-done | bytes 524320 | tf_op jit(solution)/shard_map/ppermute | solution.py:501
  25.9 1.5 collective-permute-start.5
  29.0 2.0 collective-permute-start.2
  31.1 8.1 %collective-permute-done.5.refs_7_ = bf16[64,4096]{1,0:T(8,128)(2,1)} collective-permute-done((bf16[64,4096]{1,0:T(8,128)(2,1)}, bf16[64,4096]{1,0:T(8,128)(2,1)}, u32[]{:S(2)}, u32[]{:S(2)}) %collective-permute-start.5) | collective-permute-done | bytes 524320 | tf_op jit(solution)/shard_map/ppermute | solution.py:501
  39.2 18.7 %dgrad.2 = (s16[128,4224]{1,0:T(8,128)(2,1)}, f32[128,4096]{1,0:T(8,128)}, bf16[4096,3584]{1,0:T(8,128)(2,1)}) custom-call(s32[963]{0:T(1024)} %pad_add_fusion.meta, bf16[256,3584]{1,0:T(8,128)(2,1)} %bitcast.17, bf16[256,3584]{1,0:T(8,128)(2,1)} %bitcast.18, bf16[256,3584]{1,0:T(8,128)(2,1)} %bitcast.19, bf16[256,3584]{1,0:T(8,128)(2,1)} %bitcast.20, ...), custom_call_target="tpu_custom_call" | custom-call | flops 7516192768 | bytes 35389440 | tf_op jit(solution)/shard_map/dgrad/pallas_call | solution.py:203
  57.9 6.6 %collective-permute-done.6.refs_5_ = bf16[64,4096]{1,0:T(8,128)(2,1)} collective-permute-done((bf16[64,4096]{1,0:T(8,128)(2,1)}, bf16[64,4096]{1,0:T(8,128)(2,1)}, u32[]{:S(2)}, u32[]{:S(2)}) %collective-permute-start.6) | collective-permute-done | bytes 524320 | tf_op jit(solution)/shard_map/ppermute | solution.py:501
  64.5 23.3 %forward.1 = (s16[256,3712]{1,0:T(8,128)(2,1)}, f32[256,3584]{1,0:T(8,128)}, bf16[512,4096]{1,0:T(8,128)(2,1)}) custom-call(s32[963]{0:T(1024)} %pad_add_fusion.meta, bf16[64,4096]{1,0:T(8,128)(2,1)} %bitcast.26, bf16[64,4096]{1,0:T(8,128)(2,1)} %collective-permute-done.refs_1_, bf16[64,4096]{1,0:T(8,128)(2,1)} %collective-permute-done.1.refs_2_, ...), custom_call_target="tpu_custom_call" | custom-call | flops 15032385536 | bytes 40894464 | tf_op jit(solution)/shard_map/forward/pallas_call | solution.py:203
  88.5 15.9 %dgrad.3 = (s16[128,4224]{1,0:T(8,128)(2,1)}, f32[128,4096]{1,0:T(8,128)}) custom-call(s32[963]{0:T(1024)} %pad_add_fusion.meta, bf16[256,3584]{1,0:T(8,128)(2,1)} %collective-permute-done.8.refs_0_.refs_1_.refs_2_.refs_3_, bf16[256,3584]{1,0:T(8,128)(2,1)} %collective-permute-done.8.refs_0_.refs_1_.refs_2_.refs_3_, ...), custom_call_target="tpu_custom_call" | custom-call | flops 7516192768 | bytes 35389440 | tf_op jit(solution)/shard_map/dgrad/pallas_call | solution.py:203
  104.5 1.5 collective-permute-start.10
  106.0 1.5 collective-permute-start.7
  107.5 7.6 %collective-permute-done.9.refs_4_.refs_5_.refs_6_.refs_7_ = s16[128,4224]{1,0:T(8,128)(2,1)} collective-permute-done((s16[128,4224]{1,0:T(8,128)(2,1)}, s16[128,4224]{1,0:T(8,128)(2,1)}, u32[]{:S(2)}, u32[]{:S(2)}) %collective-permute-start.9) | collective-permute-done | bytes 1081376 | tf_op jit(solution)/shard_map/ppermute | solution.py:501
  115.1 22.6 %collective-permute-done.10.refs_8_.refs_9_.refs_10_.refs_11_ = s16[128,4224]{1,0:T(8,128)(2,1)} collective-permute-done((s16[128,4224]{1,0:T(8,128)(2,1)}, s16[128,4224]{1,0:T(8,128)(2,1)}, u32[]{:S(2)}, u32[]{:S(2)}) %collective-permute-start.10) | collective-permute-done | bytes 1081376 | tf_op jit(solution)/shard_map/ppermute | solution.py:501
  137.7 7.3 %add_received.2 = (s16[64,4224]{1,0:T(8,128)(2,1)}, s16[64,4224]{1,0:T(8,128)(2,1)}, s16[64,4224]{1,0:T(8,128)(2,1)}, f32[64,4096]{1,0:T(8,128)}) custom-call(s32[963]{0:T(1024)} %pad_add_fusion.meta, f32[128,4096]{1,0:T(8,128)} %get-tuple-element.18.refs_0_.refs_1_, f32[128,4096]{1,0:T(8,128)} %get-tuple-element.18.refs_0_.refs_1_, ...), custom_call_target="tpu_custom_call" | custom-call | flops 2097152 | bytes 9437184 | tf_op jit(solution)/shard_map/add_received/pallas_call | solution.py:422
  145.3 13.8 %collective-permute-done.11.refs_1_.refs_2_ = s16[64,4224]{1,0:T(8,128)(2,1)} collective-permute-done((s16[64,4224]{1,0:T(8,128)(2,1)}, s16[64,4224]{1,0:T(8,128)(2,1)}, u32[]{:S(2)}, u32[]{:S(2)}) %collective-permute-start.11) | collective-permute-done | bytes 540704 | tf_op jit(solution)/shard_map/ppermute | solution.py:501
  159.1 1.1 collective-permute-start.12
  160.2 22.4 %collective-permute-done.12.refs_3_.refs_4_ = s16[64,4224]{1,0:T(8,128)(2,1)} collective-permute-done((s16[64,4224]{1,0:T(8,128)(2,1)}, s16[64,4224]{1,0:T(8,128)(2,1)}, u32[]{:S(2)}, u32[]{:S(2)}) %collective-permute-start.12) | collective-permute-done | bytes 540704 | tf_op jit(solution)/shard_map/ppermute | solution.py:501
  183.2 24.3 %collective-permute-done.13.refs_5_.refs_6_ = s16[64,4224]{1,0:T(8,128)(2,1)} collective-permute-done((s16[64,4224]{1,0:T(8,128)(2,1)}, s16[64,4224]{1,0:T(8,128)(2,1)}, u32[]{:S(2)}, u32[]{:S(2)}) %collective-permute-start.13) | collective-permute-done | bytes 540704 | tf_op jit(solution)/shard_map/ppermute | solution.py:501
  207.5 3.7 %add_received.3 = bf16[64,4096]{1,0:T(8,128)(2,1)} custom-call(s32[963]{0:T(1024)} %pad_add_fusion.meta, f32[64,4096]{1,0:T(8,128)} %get-tuple-element.22.refs_0_, s16[64,4224]{1,0:T(8,128)(2,1)} %collective-permute-done.11.refs_1_.refs_2_, s16[64,4224]{1,0:T(8,128)(2,1)} %collective-permute-done.11.refs_1_.refs_2_, ...), custom_call_target="tpu_custom_call" | custom-call | flops 2097152 | bytes 5505024 | tf_op jit(solution)/shard_map/add_received/pallas_call | solution.py:422
  211.2 5.4 %join_output.1 = bf16[256,3584]{1,0:T(8,128)(2,1)} custom-call(s32[963]{0:T(1024)} %pad_add_fusion.meta, f32[256,3584]{1,0:T(8,128)} %get-tuple-element.16.local_ref, s16[256,3712]{1,0:T(8,128)(2,1)} %collective-permute-done.7.codes_ref), custom_call_target="tpu_custom_call" | custom-call | flops 7340032 | bytes 7340032 | tf_op jit(solution)/shard_map/join_output/pallas_call | solution.py:628
  216.7 41.6 %wgrad.1 = f32[448,128,128]{2,1,0:T(8,128)} custom-call(s32[963]{0:T(1024)} %pad_add_fusion.meta, bf16[512,4096]{1,0:T(8,128)(2,1)} %get-tuple-element.26.refs_0_, bf16[512,4096]{1,0:T(8,128)(2,1)} %collective-permute-done.14.refs_1_, bf16[256,3584]{1,0:T(8,128)(2,1)} %bitcast.22, bf16[256,3584]{1,0:T(8,128)(2,1)} %collective-permute-done.8.refs_0_.refs_1_.refs_2_.refs_3_, ...), custom_call_target="tpu_custom_call" | custom-call | flops 30064771072 | bytes 45088768 | tf_op jit(solution)/shard_map/wgrad/pallas_call | solution.py:341
  (23 shorter events, 4.6 us)
Async XLA Ops:
  0.6 25.3 %collective-permute-start.3 = (bf16[64,4096]{1,0:T(8,128)(2,1)}, bf16[64,4096]{1,0:T(8,128)(2,1)}, u32[]{:S(2)}, u32[]{:S(2)}) collective-permute-start(bf16[64,4096]{1,0:T(8,128)(2,1)} %bitcast.23), channel_id=1, source_target_pairs={{0,12},{2,14},{4,8},{6,10},{8,4},{10,6},{12,0},{14,2},{1,13},{3,15... | collective-permute-start | bytes 1572872 | tf_op jit(solution)/shard_map/ppermute | solution.py:501
  2.3 26.8 %collective-permute-start = (bf16[64,4096]{1,0:T(8,128)(2,1)}, bf16[64,4096]{1,0:T(8,128)(2,1)}, u32[]{:S(2)}, u32[]{:S(2)}) collective-permute-start(bf16[64,4096]{1,0:T(8,128)(2,1)} %bitcast.24), channel_id=1, source_target_pairs={{0,2},{2,0},{4,6},{6,4},{8,10},{10,8},{12,14},{14,12},{1,3},{3,1},... | collective-permute-start | bytes 1572872 | tf_op jit(solution)/shard_map/ppermute | solution.py:501
  3.8 54.1 %collective-permute-start.1 = (bf16[64,4096]{1,0:T(8,128)(2,1)}, bf16[64,4096]{1,0:T(8,128)(2,1)}, u32[]{:S(2)}, u32[]{:S(2)}) collective-permute-start(bf16[64,4096]{1,0:T(8,128)(2,1)} %bitcast.25), channel_id=1, source_target_pairs={{0,4},{2,6},{4,0},{6,2},{8,12},{10,14},{12,8},{14,10},{1,5},{3,7},... | collective-permute-start | bytes 1572872 | tf_op jit(solution)/shard_map/ppermute | solution.py:501
  6.3 82.3 %collective-permute-start.8 = (bf16[256,3584]{1,0:T(8,128)(2,1)}, bf16[256,3584]{1,0:T(8,128)(2,1)}, u32[]{:S(2)}, u32[]{:S(2)}) collective-permute-start(bf16[256,3584]{1,0:T(8,128)(2,1)} %bitcast.16), channel_id=1, source_target_pairs={{0,16},{16,0},{1,17},{17,1},{2,18},{18,2},{3,19},{19,3},{4,20},{20... | collective-permute-start | bytes 5505032 | tf_op jit(solution)/shard_map/ppermute | solution.py:501
  25.9 13.3 %collective-permute-start.5 = (bf16[64,4096]{1,0:T(8,128)(2,1)}, bf16[64,4096]{1,0:T(8,128)(2,1)}, u32[]{:S(2)}, u32[]{:S(2)}) collective-permute-start(bf16[64,4096]{1,0:T(8,128)(2,1)} %collective-permute-done.3.refs_6_), channel_id=1, source_target_pairs={{0,2},{2,0},{4,6},{6,4},{8,10},{10,8},{12,14},{14,12},{1,3},{3,1},... | collective-permute-start | bytes 1572872 | tf_op jit(solution)/shard_map/ppermute | solution.py:501
  29.0 28.9 %collective-permute-start.4 = (bf16[64,4096]{1,0:T(8,128)(2,1)}, bf16[64,4096]{1,0:T(8,128)(2,1)}, u32[]{:S(2)}, u32[]{:S(2)}) collective-permute-start(bf16[64,4096]{1,0:T(8,128)(2,1)} %collective-permute-done.3.refs_6_), channel_id=1, source_target_pairs={{0,4},{2,6},{4,0},{6,2},{8,12},{10,14},{12,8},{14,10},{1,5},{3,7},... | collective-permute-start | bytes 1572872 | tf_op jit(solution)/shard_map/ppermute | solution.py:501
  29.0 28.9 %collective-permute-start.2 = (bf16[64,4096]{1,0:T(8,128)(2,1)}, bf16[64,4096]{1,0:T(8,128)(2,1)}, u32[]{:S(2)}, u32[]{:S(2)}) collective-permute-start(bf16[64,4096]{1,0:T(8,128)(2,1)} %collective-permute-done.refs_1_), channel_id=1, source_target_pairs={{0,4},{2,6},{4,0},{6,2},{8,12},{10,14},{12,8},{14,10},{1,5},{3,7},... | collective-permute-start | bytes 1572872 | tf_op jit(solution)/shard_map/ppermute | solution.py:501
  39.2 25.3 %collective-permute-start.6 = (bf16[64,4096]{1,0:T(8,128)(2,1)}, bf16[64,4096]{1,0:T(8,128)(2,1)}, u32[]{:S(2)}, u32[]{:S(2)}) collective-permute-start(bf16[64,4096]{1,0:T(8,128)(2,1)} %collective-permute-done.5.refs_7_), channel_id=1, source_target_pairs={{0,4},{2,6},{4,0},{6,2},{8,12},{10,14},{12,8},{14,10},{1,5},{3,7},... | collective-permute-start | bytes 1572872 | tf_op jit(solution)/shard_map/ppermute | solution.py:501
  87.9 128.8 %collective-permute-start.14 = (bf16[512,4096]{1,0:T(8,128)(2,1)}, bf16[512,4096]{1,0:T(8,128)(2,1)}, u32[]{:S(2)}, u32[]{:S(2)}) collective-permute-start(bf16[512,4096]{1,0:T(8,128)(2,1)} %get-tuple-element.26.refs_0_), channel_id=1, source_target_pairs={{0,1},{1,0},{2,3},{3,2},{4,5},{5,4},{6,7},{7,6},{8,9},{9,8},{10,11... | collective-permute-start | bytes 12582920 | tf_op jit(solution)/shard_map/ppermute | solution.py:501
  88.0 27.1 %collective-permute-start.9 = (s16[128,4224]{1,0:T(8,128)(2,1)}, s16[128,4224]{1,0:T(8,128)(2,1)}, u32[]{:S(2)}, u32[]{:S(2)}) collective-permute-start(s16[128,4224]{1,0:T(8,128)(2,1)} %get-tuple-element.20), channel_id=1, source_target_pairs={{0,2},{2,0},{4,6},{6,4},{8,10},{10,8},{12,14},{14,12},{1,3},{3,1},... | collective-permute-start | bytes 3244040 | tf_op jit(solution)/shard_map/ppermute | solution.py:501
  104.5 33.2 %collective-permute-start.10 = (s16[128,4224]{1,0:T(8,128)(2,1)}, s16[128,4224]{1,0:T(8,128)(2,1)}, u32[]{:S(2)}, u32[]{:S(2)}) collective-permute-start(s16[128,4224]{1,0:T(8,128)(2,1)} %get-tuple-element.21), channel_id=1, source_target_pairs={{0,2},{2,0},{4,6},{6,4},{8,10},{10,8},{12,14},{14,12},{1,3},{3,1},... | collective-permute-start | bytes 3244040 | tf_op jit(solution)/shard_map/ppermute | solution.py:501
  106.0 105.2 %collective-permute-start.7 = (s16[256,3712]{1,0:T(8,128)(2,1)}, s16[256,3712]{1,0:T(8,128)(2,1)}, u32[]{:S(2)}, u32[]{:S(2)}) collective-permute-start(s16[256,3712]{1,0:T(8,128)(2,1)} %get-tuple-element.17), channel_id=1, source_target_pairs={{0,16},{16,0},{1,17},{17,1},{2,18},{18,2},{3,19},{19,3},{4,20},{20... | collective-permute-start | bytes 5701640 | tf_op jit(solution)/shard_map/ppermute | solution.py:501
  107.5 109.1 %collective-permute-start.15 = (bf16[256,3584]{1,0:T(8,128)(2,1)}, bf16[256,3584]{1,0:T(8,128)(2,1)}, u32[]{:S(2)}, u32[]{:S(2)}) collective-permute-start(bf16[256,3584]{1,0:T(8,128)(2,1)} %bitcast.21), channel_id=1, source_target_pairs={{0,1},{1,0},{2,3},{3,2},{4,5},{5,4},{6,7},{7,6},{8,9},{9,8},{10,11... | collective-permute-start | bytes 5505032 | tf_op jit(solution)/shard_map/ppermute | solution.py:501
  115.1 101.6 %collective-permute-start.16 = (bf16[256,3584]{1,0:T(8,128)(2,1)}, bf16[256,3584]{1,0:T(8,128)(2,1)}, u32[]{:S(2)}, u32[]{:S(2)}) collective-permute-start(bf16[256,3584]{1,0:T(8,128)(2,1)} %collective-permute-done.8.refs_0_.refs_1_.refs_2_.refs_3_), channel_id=1, source_target_pairs={{0,1},{1,0},{2,3},{3,2},{4,5},{5,4},{6,7},{7,6},{8,9},{9,8},{10,11... | collective-permute-start | bytes 5505032 | tf_op jit(solution)/shard_map/ppermute | solution.py:501
  145.0 14.1 %collective-permute-start.11 = (s16[64,4224]{1,0:T(8,128)(2,1)}, s16[64,4224]{1,0:T(8,128)(2,1)}, u32[]{:S(2)}, u32[]{:S(2)}) collective-permute-start(s16[64,4224]{1,0:T(8,128)(2,1)} %get-tuple-element.23), channel_id=1, source_target_pairs={{0,4},{2,6},{4,0},{6,2},{8,12},{10,14},{12,8},{14,10},{1,5},{3,7},... | collective-permute-start | bytes 1622024 | tf_op jit(solution)/shard_map/ppermute | solution.py:501
  159.1 23.5 %collective-permute-start.12 = (s16[64,4224]{1,0:T(8,128)(2,1)}, s16[64,4224]{1,0:T(8,128)(2,1)}, u32[]{:S(2)}, u32[]{:S(2)}) collective-permute-start(s16[64,4224]{1,0:T(8,128)(2,1)} %get-tuple-element.24), channel_id=1, source_target_pairs={{0,8},{2,10},{4,12},{6,14},{8,0},{10,2},{12,4},{14,6},{1,9},{3,11}... | collective-permute-start | bytes 1622024 | tf_op jit(solution)/shard_map/ppermute | solution.py:501
  182.7 24.8 %collective-permute-start.13 = (s16[64,4224]{1,0:T(8,128)(2,1)}, s16[64,4224]{1,0:T(8,128)(2,1)}, u32[]{:S(2)}, u32[]{:S(2)}) collective-permute-start(s16[64,4224]{1,0:T(8,128)(2,1)} %get-tuple-element.25), channel_id=1, source_target_pairs={{0,12},{2,14},{4,8},{6,10},{8,4},{10,6},{12,0},{14,2},{1,13},{3,15... | collective-permute-start | bytes 1622024 | tf_op jit(solution)/shard_map/ppermute | solution.py:501
